TPU v7x, 128 devices: a whole 4x4x4 slice. The times are simulated.
128 devices in a mesh: grp: 8 (over x, y_hi), dev: 16 (over y_lo, z, core).
Axes of the slice: x: 4, y: 4 (y_hi: 2, y_lo: 2; y = y_hi * 2 + y_lo), z: 4, core: 2. Of those that a mesh axis runs over, the one named last changes fastest.
Arguments:
- batch_rows: bfloat16 [4096, 512], P(('grp', 'dev')), may hold values from -30 to 30
- batch_labels: int32 [4096], P(('grp', 'dev')), may hold values from 0 to 1023, as said below
- memory: bfloat16 [262144, 512], P(('grp', 'dev')), may hold values from -30 to 30
- memory_labels: int32 [262144], P(('grp', 'dev')), may hold values from 0 to 1023
- keep_bits: int32 [262144], P(('grp', 'dev')), may hold values from 0 to 1
- step_index: int32 [1], replicated, may hold values from 0 to 999999
Outputs:
- grad_batch: float32 [4096, 512], P(('grp', 'dev'))
- anchor_loss: float32 [4096], P(('grp', 'dev'))
- new_memory: bfloat16 [262144, 512], P(('grp', 'dev'))
- new_labels: int32 [262144], P(('grp', 'dev'))
Inputs may be any that keep to these rules, and one draw needn't show every extreme that they name: `batch_labels`: labels of batch and memory rows are class numbers below 1024.
All inputs are finite; a program needn't handle non-finite values.
Results may differ from a plain program's by a relative error of at most 0.0034.
Values may be sent and summed in bfloat16 or wider, within the bound.
A program may use at most 128 MiB of HBM per device.

v0:
```python
import jax
import jax.numpy as jnp
from jax import lax
from jax.sharding import PartitionSpec as P

pos_scale = 2.0
neg_scale = 50.0
margin = 0.5


def normalize(values):
    floats = values.astype(jnp.float32)
    radius = jnp.sqrt(jnp.sum(floats * floats, axis=1, keepdims=True) + 1e-06)
    return (floats / radius, radius)


def per_device(batch_rows, batch_labels, memory, memory_labels, keep_bits, step_index):
    group_size = lax.axis_size("dev")
    devices_all = lax.axis_size("grp") * group_size
    my_index = lax.axis_index("grp") * group_size + lax.axis_index("dev")
    local_rows = batch_rows.shape[0]
    width = batch_rows.shape[1]
    unit_rows, radius = normalize(batch_rows)
    local_anchors = unit_rows.astype(jnp.bfloat16)
    anchors, labels_all = (
        lax.all_gather(local_anchors, ("grp", "dev"), axis=0, tiled=True),
        lax.all_gather(batch_labels, ("grp", "dev"), axis=0, tiled=True),
    )
    memory_keys = normalize(memory)[0].astype(jnp.bfloat16)
    kept_rows = (keep_bits > 0)[None, :]
    row_count = anchors.shape[0]
    block_rows = min(512, row_count)
    blocks = row_count // block_rows

    def score_block(inputs):
        block_anchors, block_labels = inputs
        scores = lax.dot_general(
            block_anchors, memory_keys, (((1,), (1,)), ((), ())), preferred_element_type=jnp.float32
        )
        same_class = block_labels[:, None] == memory_labels[None, :]
        positive = jnp.logical_and(same_class, kept_rows)
        negative = jnp.logical_and(jnp.logical_not(same_class), kept_rows)
        pos_term = jnp.where(positive, jnp.exp(-pos_scale * (scores - margin)), 0.0)
        neg_term = jnp.where(negative, jnp.exp(neg_scale * (scores - margin)), 0.0)
        pull = jnp.dot(
            pos_term.astype(jnp.bfloat16), memory_keys, preferred_element_type=jnp.float32
        )
        push = jnp.dot(
            neg_term.astype(jnp.bfloat16), memory_keys, preferred_element_type=jnp.float32
        )
        return (jnp.sum(pos_term, axis=1), jnp.sum(neg_term, axis=1), pull, push)

    pos_sum, neg_sum, pull, push = lax.map(
        score_block,
        (anchors.reshape(blocks, block_rows, width), labels_all.reshape(blocks, block_rows)),
    )
    pos_sum = pos_sum.reshape(row_count)
    neg_sum = neg_sum.reshape(row_count)
    pull = pull.reshape(row_count, width)
    push = push.reshape(row_count, width)
    pos_total, neg_total = lax.psum((pos_sum, neg_sum), ("grp", "dev"))
    combined = push / (1.0 + neg_total)[:, None] - pull / (1.0 + pos_total)[:, None]
    grad_unit = lax.psum_scatter(combined, ("grp", "dev"), scatter_dimension=0, tiled=True)
    own_pos = lax.dynamic_slice_in_dim(pos_total, my_index * local_rows, local_rows, 0)
    own_neg = lax.dynamic_slice_in_dim(neg_total, my_index * local_rows, local_rows, 0)
    anchor_loss = jnp.log(1.0 + own_pos) / pos_scale + jnp.log(1.0 + own_neg) / neg_scale
    along = jnp.sum(unit_rows * grad_unit, axis=1, keepdims=True)
    grad_batch = (grad_unit - unit_rows * along) / radius
    step_value = step_index[0]
    slot_index = step_value % (memory.shape[0] // local_rows)
    source = (my_index - step_value) % devices_all
    moved_rows = lax.dynamic_slice_in_dim(anchors, source * local_rows, local_rows, 0)
    moved_labels = lax.dynamic_slice_in_dim(labels_all, source * local_rows, local_rows, 0)
    new_memory = lax.dynamic_update_slice_in_dim(memory, moved_rows, slot_index * local_rows, 0)
    new_labels = lax.dynamic_update_slice_in_dim(
        memory_labels, moved_labels, slot_index * local_rows, 0
    )
    return (grad_batch, anchor_loss, new_memory, new_labels)


def solution(mesh):
    placed = (
        P(("grp", "dev"), None),
        P(("grp", "dev")),
        P(("grp", "dev"), None),
        P(("grp", "dev")),
        P(("grp", "dev")),
        P(),
    )
    return jax.shard_map(
        per_device,
        mesh=mesh,
        in_specs=placed,
        out_specs=(
            P(("grp", "dev"), None),
            P(("grp", "dev")),
            P(("grp", "dev"), None),
            P(("grp", "dev")),
        ),
        check_vma=False,
    )
```

profile of v0, /device:TPU:0, one launch (start us, length us, event | category | flops | bytes accessed | tf_op | source)
XLA Modules:
  0.0 900.4 jit_solution(15822129743591129531)
XLA Ops:
  7.2 1.6 copy.37
  10.1 68.7 %all-reduce = s32[4096]{0:T(1024)S(1)} all-reduce(s32[4096]{0:T(1024)S(1)} %dynamic-update-slice), channel_id=1, replica_groups=mesh['grp'=8,'dev'=16] {'grp','dev'}, use_global_device_ids=true, to_apply=%add | all-reduce | flops 4096 | bytes 32768
  79.3 1.8 fusion.41
  81.1 81.6 %while.18 = (s32[]{:T(128)}, f32[8,512]{1,0:T(8,128)S(1)}, f32[8,512]{1,0:T(8,128)S(1)}, f32[8,512,512]{2,1,0:T(8,128)}, f32[8,512,512]{2,1,0:T(8,128)}, /*index...) while((s32[]{:T(128)}, f32[8,512]{1,0:T(8,128)S(1)}, ...), condition=%wide.region_5.6_spmd, body=%wide.region_2.5_spmd.sunk | while | flops 3246390272 | bytes 29943460 | solution.py:53
  81.2 5.1 fusion.60
  86.3 2.5 fusion.61
  88.8 2.5 fusion.62
  91.5 5.1 fusion.60
  96.6 2.4 fusion.61
  98.9 2.5 fusion.62
  101.7 5.1 fusion.60
  106.8 2.4 fusion.61
  109.1 2.5 fusion.62
  111.8 5.1 fusion.60
  117.0 2.4 fusion.61
  119.3 2.5 fusion.62
  122.0 5.1 fusion.60
  127.1 2.4 fusion.61
  129.6 2.5 fusion.62
  132.2 5.1 fusion.60
  137.3 2.4 fusion.61
  139.7 2.5 fusion.62
  142.4 5.1 fusion.60
  147.5 2.4 fusion.61
  149.9 2.5 fusion.62
  152.6 5.1 fusion.60
  157.7 2.4 fusion.61
  160.1 2.5 fusion.62
  162.8 63.2 %all-reduce.1 = (f32[4096]{0:T(1024)S(1)}, f32[4096]{0:T(1024)S(1)}) all-reduce(f32[4096]{0:T(1024)S(1)} %bitcast.56, f32[4096]{0:T(1024)S(1)} %bitcast.55), channel_id=1, replica_groups=mesh['grp'=8,'dev'=16] {'grp','dev'}, use_global_device_ids=true, to_apply=%region_7.8 | all-reduce | flops 8192 | bytes 65536 | tf_op jit(solution)/shard_map/psum | solution.py:61
  225.9 10.1 %fusion.39 = f32[4096,512]{1,0:T(8,128)} fusion(f32[8,512,512]{2,1,0:T(8,128)} %get-tuple-element.134, f32[8,512,512]{2,1,0:T(8,128)} %get-tuple-element.132, f32[4096]{0:T(1024)S(1)} %get-tuple-element.161, f32[4096]{0:T(1024)S(1)} %get-tuple-element.162), kind=kLoop, calls=%fused_computation.35 | loop fusion | flops 6291456 | bytes 25198592 | tf_op jit(solution)/shard_map/sub | solution.py:62
  238.2 652.8 %reduce-scatter.2.cloned.1.call-done = f32[32,512]{1,0:T(8,128)} async-done(((f32[4096,512]{1,0:T(8,128)}), f32[32,512]{1,0:T(8,128)}) %reduce-scatter.2.cloned.1.call-update) | async-done | bytes 65552 | tf_op jit(solution)/shard_map/reduce_scatter | solution.py:63
  892.0 1.6 subtract_divide_fusion
  (86 shorter events, 5.5 us)
Async XLA Ops:
  7.2 1.7 copy-start.2
  7.2 2.6 copy-start.6
  7.2 71.6 %copy-start.3 = (s32[2048]{0:T(1024)S(1)}, s32[2048]{0:T(1024)}, u32[]{:S(2)}) copy-start(s32[2048]{0:T(1024)} %param.12) | copy-start | bytes 24580
  7.2 73.9 %all-gather.2.cloned.1.call-start = ((), (), s32[]{:S(2)}) async-start(), calls=%async_computation.1 | async-start | bytes 4227072 | tf_op jit(solution)/shard_map/all_gather | solution.py:26
  8.8 72.3 %copy-start.5 = (s32[2048]{0:T(1024)S(1)}, s32[2048]{0:T(1024)}, u32[]{:S(2)}) copy-start(s32[2048]{0:T(1024)} %param.11) | copy-start | bytes 24580
  9.7 881.3 %reduce-scatter.2.cloned.1.call-start = ((), (), s32[]{:S(2)}) async-start(), calls=%async_computation.2 | async-start | bytes 8454144 | tf_op jit(solution)/shard_map/reduce_scatter | solution.py:63
  81.2 5.1 copy-start.1
  91.4 5.1 copy-start.1
  101.7 5.1 copy-start.1
  111.8 5.1 copy-start.1
  122.0 5.1 copy-start.1
  132.2 5.1 copy-start.1
  142.4 5.1 copy-start.1
  152.6 5.1 copy-start.1
  237.5 656.2 %copy-start.4 = (s32[2048]{0:T(1024)}, s32[2048]{0:T(1024)S(1)}, u32[]{:S(2)}) copy-start(s32[2048]{0:T(1024)S(1)} %dynamic-slice_dynamic-update-slice_fusion.1) | copy-start | bytes 24580
  238.2 655.4 %copy-start = (bf16[2048,512]{1,0:T(8,128)(2,1)}, bf16[2048,512]{1,0:T(8,128)(2,1)S(1)}, u32[]{:S(2)}) copy-start(bf16[2048,512]{1,0:T(8,128)(2,1)S(1)} %dynamic-slice_dynamic-update-slice_fusion) | copy-start | bytes 6291460
Sparse Core Ops, SparseCore 0:
  11.7 69.2 all-gather.1
  236.1 654.8 reduce-scatter.1
where the time goes:
time: 901 us; the launch traced here: 900 us
  waiting for transfers between devices  653 us (72%)
  blocking collectives  132 us (15%)
  matrix products  80 us (9%)
  other arithmetic  16.7 us (2%)
  between operations  14.9 us (2%)
    reduce_scatter x1, waiting for transfers between devices, per_device(): lax.psum_scatter(combined, ('grp', 'dev'), scatter_dimension=0, tiled=True)  653 us
    unnamed x1, blocking collectives  68.7 us
    psum x1, blocking collectives, per_device(): pos_total, neg_total = lax.psum((pos_sum, neg_sum), ('grp', 'dev'))  63.2 us
    dot_general x8, matrix products, score_block(): lax.dot_general(block_anchors, memory_keys, (((1,), (1,)), ((), ())), pre...  40.9 us
    dot_general x8, matrix products, score_block(): jnp.dot(neg_term.astype(jnp.bfloat16), memory_keys, preferred_element_typ...  20.1 us
    dot_general x8, matrix products, score_block(): jnp.dot(pos_term.astype(jnp.bfloat16), memory_keys, preferred_element_typ...  19.1 us
  transfers between devices with their start and end apart: 2, of which 1 were waited for; matrix products, arithmetic and copies ran while one was open for 0% of the time, Pallas kernels for 0%

commit v1 on v0

v1 whole, which is shorter than its diff:
```python
import functools
import math

import jax
import jax.numpy as jnp
from jax import lax
from jax.experimental import pallas as pl
from jax.experimental.pallas import tpu as pltpu
from jax.sharding import PartitionSpec as P

F32, BF16, I32 = jnp.float32, jnp.bfloat16, jnp.int32
MESH = pl.DeviceIdType.MESH
LOG2E = math.log2(math.e)
EXP_NEG = math.exp(-25.0)
EXP_POS = math.exp(1.0)

ORDERS = ((0, 1, 2), (2, 0, 1))
STRIDES = (16, 4, 1)
ROWS = 16
CHUNK = 256
WIDTH = 512
KEYS_DEV = 2048
KEYS = 4096
S_TILE = 2048
VISIT = (0, 1, 3, 2)


def column(row):
    return jnp.transpose(jnp.broadcast_to(row, (128, 128)))


def unit_scale(values):
    return lax.rsqrt(jnp.sum(values * values, axis=1, keepdims=True) + 1e-06)


def kernel(
    step_ref, batch_ref, blab_ref, mlab_ref, keep_ref, mem_ref,
    grad_ref, loss_ref, moved_ref, mvlab_ref, newmem_ref,
    mraw, klraw, kpraw, keys, klab, raw, labs, an, labc, terms, acc, sums, sums_in, den,
    gpart, gown, sb1, rb1, g1, sb2, rb2, g2, sb3, rb3, cand, cand_in, clab, clab_in,
    mem_sem, out_sem, agd_s, agd_r, agl_s, agl_r, ar_s, ar_r, rs_s, rs_r, pt_s, pt_r, bt_s, bt_r,
):
    n_dev = lax.axis_size("dev")
    me = lax.axis_index("grp") * n_dev + lax.axis_index("dev")
    core = me % 2
    chip = me // 2
    at = (chip // 16, (chip // 4) % 4, chip % 4)

    def device(index):
        return (index // n_dev, index % n_dev)

    def peer(axis, off):
        there = (at[axis] + off) % 4
        return device(me + (there - at[axis]) * (2 * STRIDES[axis]))

    partner = device(me + 1 - 2 * core)

    def remote(src, dst, send, recv, to):
        return pltpu.make_async_remote_copy(
            src_ref=src, dst_ref=dst, send_sem=send, recv_sem=recv, device_id=to, device_id_type=MESH
        )

    own_mem = pltpu.make_async_copy(mem_ref, mraw.at[0], mem_sem)
    own_mem.start()

    barrier = pltpu.get_barrier_semaphore()
    for axis in range(3):
        for off in (1, 2, 3):
            pl.semaphore_signal(barrier, inc=1, device_id=peer(axis, off), device_id_type=MESH)
    pl.semaphore_signal(barrier, inc=1, device_id=partner, device_id_type=MESH)
    for p, (f, m, l) in enumerate(ORDERS):
        raw[p, at[l], at[m], at[f]] = batch_ref[pl.ds(p * ROWS, ROWS), :]
        labs[p, at[l], at[m], at[f]] = blab_ref[...]
    pl.semaphore_wait(barrier, 10)

    def slot(ref, p, phase, off):
        f, m, l = (at[a] for a in ORDERS[p])
        if phase == 0:
            return ref.at[p, l, m, (f + off) % 4]
        if phase == 1:
            return ref.at[p, l, (m + off) % 4]
        return ref.at[p, (l + off) % 4]

    def gather(p, phase, off, back):
        shift = 4 - off if back else 0
        to = peer(ORDERS[p][phase], off)
        rows, labels = slot(raw, p, phase, shift), slot(labs, p, phase, shift)
        return (
            remote(rows, rows, agd_s.at[p, phase, off - 1], agd_r.at[p, phase, off - 1], to),
            remote(labels, labels, agl_s.at[p, phase, off - 1], agl_r.at[p, phase, off - 1], to),
        )

    def gather_start(phase):
        for off in (1, 3, 2):
            for p in (0, 1):
                for copy in gather(p, phase, off, False):
                    copy.start()

    def gather_recv(phase):
        for p in (0, 1):
            for off in (1, 2, 3):
                for copy in gather(p, phase, off, True):
                    copy.wait_recv()

    gather_start(0)
    swaps = (
        remote(mem_ref, mraw.at[1], pt_s.at[0], pt_r.at[0], partner),
        remote(mlab_ref, klraw.at[1], pt_s.at[1], pt_r.at[1], partner),
        remote(keep_ref, kpraw.at[1], pt_s.at[2], pt_r.at[2], partner),
    )
    for copy in swaps:
        copy.start()

    klraw[0] = mlab_ref[...]
    kpraw[0] = keep_ref[...]

    def normalize_memory(half):
        def block(i, _):
            row = pl.multiple_of(i * 128, 128)
            kept = kpraw[half, :, pl.ds(row, 128)] > 0
            klab[half, :, pl.ds(row, 128)] = jnp.where(
                kept, klraw[half, :, pl.ds(row, 128)], -1
            ).astype(F32)
            values = mraw[half, pl.ds(row, 128), :].astype(F32)
            scale = unit_scale(values) * column(jnp.where(kept, 1.0, 0.0))[:, 0:1]
            keys[pl.ds(pl.multiple_of(half * KEYS_DEV + row, 128), 128), :] = (values * scale).astype(BF16)
            return 0

        lax.fori_loop(0, KEYS_DEV // 128, block, 0)

    own_mem.wait()
    out_mem = pltpu.make_async_copy(mraw.at[0], newmem_ref, out_sem)
    out_mem.start()
    normalize_memory(0)
    gather_recv(0)
    gather_start(1)
    for copy in swaps:
        copy.wait_recv()
    normalize_memory(1)
    gather_recv(1)
    gather_start(2)

    dropped = float(KEYS) - jnp.sum(
        jnp.where(kpraw[...] > 0, 1.0, 0.0).reshape(2, KEYS_DEV), axis=(0, 1), keepdims=True
    )

    def prepare(p, l):
        values = raw[p, l].reshape(CHUNK, WIDTH).astype(F32)
        an[p, l] = (values * unit_scale(values)).astype(BF16)
        pages = labs[p, l].reshape(16, 128).astype(F32)
        wide = jnp.transpose(jnp.concatenate([pages] * 8, axis=0))
        for b in range(16):
            labc[p, l, pl.ds(b * ROWS, ROWS), :] = jnp.broadcast_to(
                wide[p * ROWS : (p + 1) * ROWS, b : b + 1], (ROWS, 128)
            )

    def score(p, l):
        acc[...] = jnp.zeros_like(acc)

        def tile(t, _):
            first = pl.multiple_of(t * S_TILE, S_TILE)
            s = lax.dot_general(
                an[p, l], keys[pl.ds(first, S_TILE), :], (((1,), (1,)), ((), ())),
                preferred_element_type=F32,
            )
            labels = labc[p, l]
            all_sum, pos_sum = acc[0], acc[1]
            for j in range(S_TILE // 128):
                sj = s[:, j * 128 : (j + 1) * 128]
                same = labels == klab[t, :, j * 128 : (j + 1) * 128]
                e = jnp.exp2(sj * jnp.where(same, -2.0 * LOG2E, 50.0 * LOG2E))
                all_sum = all_sum + e
                pos_sum = pos_sum + jnp.where(same, e, 0.0)
                terms[p, l, :, pl.ds(pl.multiple_of(first + j * 128, 128), 128)] = e.astype(BF16)
            acc[0], acc[1] = all_sum, pos_sum
            return 0

        lax.fori_loop(0, KEYS // S_TILE, tile, 0)
        for h in (0, 1):
            half = pl.ds(h * 128, 128)
            total = jnp.sum(jnp.transpose(acc[0, half, :]), axis=0, keepdims=True)
            pos = jnp.sum(jnp.transpose(acc[1, half, :]), axis=0, keepdims=True)
            sums[0, p, l, h : h + 1, :] = total - pos - dropped
            sums[0, p, l, 2 + h : 3 + h, :] = pos

    def visit(i, _):
        off = jnp.where(i == 2, 3, jnp.where(i == 3, 2, i))
        for p in (0, 1):
            f, m, l = (at[a] for a in ORDERS[p])
            here = (l + 4 - off) % 4

            @pl.when(off > 0)
            def _():
                to = peer(ORDERS[p][2], 1)
                k = jnp.maximum(off - 1, 0)
                rows, labels = raw.at[p, here], labs.at[p, here]
                remote(rows, rows, agd_s.at[p, 2, k], agd_r.at[p, 2, k], to).wait_recv()
                remote(labels, labels, agl_s.at[p, 2, k], agl_r.at[p, 2, k], to).wait_recv()

            prepare(p, here)
            score(p, here)
        return 0

    lax.fori_loop(0, 4, visit, 0)

    for phase in range(3):
        copies = [
            remote(
                sums.at[phase], sums_in.at[phase, off - 1],
                ar_s.at[phase, off - 1], ar_r.at[phase, off - 1], peer(phase, off),
            )
            for off in (1, 2, 3)
        ]
        for copy in copies:
            copy.start()
        for copy in copies:
            copy.wait_recv()
        sums[phase + 1] = (
            sums[phase] + sums_in[phase, 0] + sums_in[phase, 1] + sums_in[phase, 2]
        )
        for copy in copies:
            copy.wait_send()

    def ring1(p, off):
        k = off - 1
        return remote(
            sb1.at[p, k], rb1.at[p, k], rs_s.at[p, 0, k], rs_r.at[p, 0, k], peer(ORDERS[p][2], off)
        )

    def grads(p, l):
        for h in (0, 1):
            half = pl.ds(h * 128, 128)
            den[p, l, 0, half, :] = column(1.0 + EXP_NEG * sums[3, p, l, h : h + 1, :])
            den[p, l, 1, half, :] = column(1.0 + EXP_POS * sums[3, p, l, 2 + h : 3 + h, :])
        gpart[...] = jnp.zeros_like(gpart)
        labels = labc[p, l]
        neg = EXP_NEG / den[p, l, 0]
        pos = -EXP_POS / den[p, l, 1]

        def tile(t, _):
            first = pl.multiple_of(t * S_TILE, S_TILE)
            parts = []
            for j in range(S_TILE // 128):
                e = terms[p, l, :, pl.ds(pl.multiple_of(first + j * 128, 128), 128)].astype(F32)
                same = labels == klab[t, :, j * 128 : (j + 1) * 128]
                parts.append((e * jnp.where(same, pos, neg)).astype(BF16))
            gpart[...] += jnp.dot(
                jnp.concatenate(parts, axis=1), keys[pl.ds(first, S_TILE), :],
                preferred_element_type=F32,
            )
            return 0

        lax.fori_loop(0, KEYS // S_TILE, tile, 0)

    def push(i, _):
        off = jnp.where(i == 0, 2, jnp.where(i == 1, 1, 3))
        for p in (0, 1):
            l = (at[ORDERS[p][2]] + off) % 4
            grads(p, l)
            sb1[p, off - 1] = gpart[...].astype(BF16)
            ring1(p, off).start()
        return 0

    lax.fori_loop(0, 3, push, 0)
    for p in (0, 1):
        grads(p, at[ORDERS[p][2]])
        gown[p] = gpart[...]

    step = step_ref[0]
    odd = step % 2
    mate = me + 1 - 2 * core
    asker = jnp.where(odd == 0, me, mate)
    block = ((asker + 1048576 - step) % 128) // 2
    wanted = jnp.full((ROWS, WIDTH), block, I32)
    wanted_row = jnp.full((1, 128), block, I32)

    def find(q, found):
        qx, qy, qz = q // 16, (q // 4) % 4, q % 4
        pick = wanted == q
        upper = an[0, qz, pl.ds(pl.multiple_of((qy * 4 + qx) * ROWS, ROWS), ROWS), :].astype(F32)
        lower = an[1, qy, pl.ds(pl.multiple_of((qx * 4 + qz) * ROWS, ROWS), ROWS), :].astype(F32)
        return (
            jnp.where(pick, upper, found[0]),
            jnp.where(pick, lower, found[1]),
            jnp.where(wanted_row == q, labs[0, qz, qy, qx], found[2]),
        )

    nothing = jnp.zeros((ROWS, WIDTH), F32)
    upper, lower, label_row = lax.fori_loop(
        0, 64, find, (nothing, nothing, jnp.zeros((1, 128), I32))
    )
    cand[pl.ds(0, ROWS), :] = upper.astype(BF16)
    cand[pl.ds(ROWS, ROWS), :] = lower.astype(BF16)
    clab[...] = label_row
    trade = (
        remote(cand, cand_in, bt_s.at[0], bt_r.at[0], partner),
        remote(clab, clab_in, bt_s.at[1], bt_r.at[1], partner),
    )
    for copy in trade:
        copy.start()

    def ring2(p, off):
        return remote(
            sb2.at[p, off - 1], rb2.at[p, off - 1], rs_s.at[p, 1, off - 1], rs_r.at[p, 1, off - 1],
            peer(ORDERS[p][1], off),
        )

    def ring3(p, off):
        return remote(
            sb3.at[p, off - 1], rb3.at[p, off - 1], rs_s.at[p, 2, off - 1], rs_r.at[p, 2, off - 1],
            peer(ORDERS[p][0], off),
        )

    for p in (0, 1):
        m = at[ORDERS[p][1]]
        for off in (1, 2, 3):
            ring1(p, off).wait_recv()
        g1[p] = (
            gown[p] + rb1[p, 0].astype(F32) + rb1[p, 1].astype(F32) + rb1[p, 2].astype(F32)
        ).reshape(4, 64, WIDTH)
        for off in (1, 2, 3):
            sb2[p, off - 1] = g1[p, (m + off) % 4].astype(BF16)
            ring2(p, off).start()
    for p in (0, 1):
        f, m = at[ORDERS[p][0]], at[ORDERS[p][1]]
        for off in (1, 2, 3):
            ring2(p, off).wait_recv()
        g2[p] = (
            g1[p, m] + rb2[p, 0].astype(F32) + rb2[p, 1].astype(F32) + rb2[p, 2].astype(F32)
        ).reshape(4, ROWS, WIDTH)
        for off in (1, 2, 3):
            sb3[p, off - 1] = g2[p, (f + off) % 4]
            ring3(p, off).start()
    for p in (0, 1):
        f, m, l = (at[a] for a in ORDERS[p])
        for off in (1, 2, 3):
            ring3(p, off).wait_recv()
        grad_unit = g2[p, f] + rb3[p, 0] + rb3[p, 1] + rb3[p, 2]
        values = batch_ref[pl.ds(p * ROWS, ROWS), :].astype(F32)
        radius = jnp.sqrt(jnp.sum(values * values, axis=1, keepdims=True) + 1e-06)
        unit = values / radius
        along = jnp.sum(unit * grad_unit, axis=1, keepdims=True)
        mine = pl.ds(p * ROWS, ROWS)
        grad_ref[mine, :] = (grad_unit - unit * along) / radius
        own = pl.ds(pl.multiple_of((m * 4 + f) * ROWS, ROWS), ROWS)
        loss_ref[mine, :] = jnp.log(den[p, l, 1, own, :]) / 2.0 + jnp.log(den[p, l, 0, own, :]) / 50.0

    for copy in trade:
        copy.wait_recv()
    keep_mine = jnp.full((2 * ROWS, WIDTH), odd, I32) == 0
    moved_ref[...] = jnp.where(keep_mine, cand[...].astype(F32), cand_in[...].astype(F32)).astype(BF16)
    mvlab_ref[...] = jnp.where(jnp.full((1, 128), odd, I32) == 0, clab[...], clab_in[...])

    out_mem.wait()
    for copy in swaps + trade:
        copy.wait_send()
    for p in (0, 1):
        for off in (1, 2, 3):
            for phase in range(3):
                for copy in gather(p, phase, off, False):
                    copy.wait_send()
            for ring in (ring1, ring2, ring3):
                ring(p, off).wait_send()


def per_device(batch_rows, batch_labels, memory, memory_labels, keep_bits, step_index):
    local_rows = batch_rows.shape[0]
    vmem = pl.BlockSpec(memory_space=pltpu.VMEM)
    dma = pltpu.SemaphoreType.DMA
    labels = jnp.pad(batch_labels, (0, 128 - local_rows)).reshape(1, 128)
    grad, loss, moved, moved_labels, kept_memory = pl.pallas_call(
        kernel,
        out_shape=(
            jax.ShapeDtypeStruct((local_rows, WIDTH), F32),
            jax.ShapeDtypeStruct((local_rows, 128), F32),
            jax.ShapeDtypeStruct((local_rows, WIDTH), BF16),
            jax.ShapeDtypeStruct((1, 128), I32),
            jax.ShapeDtypeStruct((KEYS_DEV, WIDTH), BF16),
        ),
        in_specs=[pl.BlockSpec(memory_space=pltpu.SMEM), vmem, vmem, vmem, vmem, pl.BlockSpec(memory_space=pl.ANY)],
        out_specs=(vmem, vmem, vmem, vmem, pl.BlockSpec(memory_space=pl.ANY)),
        scratch_shapes=[
            pltpu.VMEM((2, KEYS_DEV, WIDTH), BF16),
            pltpu.VMEM((2, 1, KEYS_DEV), I32),
            pltpu.VMEM((2, 1, KEYS_DEV), I32),
            pltpu.VMEM((KEYS, WIDTH), BF16),
            pltpu.VMEM((2, 1, KEYS_DEV), F32),
            pltpu.VMEM((2, 4, 4, 4, ROWS, WIDTH), BF16),
            pltpu.VMEM((2, 4, 4, 4, 1, 128), I32),
            pltpu.VMEM((2, 4, CHUNK, WIDTH), BF16),
            pltpu.VMEM((2, 4, CHUNK, 128), F32),
            pltpu.VMEM((2, 4, CHUNK, KEYS), BF16),
            pltpu.VMEM((2, CHUNK, 128), F32),
            pltpu.VMEM((4, 2, 4, 4, 128), F32),
            pltpu.VMEM((3, 3, 2, 4, 4, 128), F32),
            pltpu.VMEM((2, 4, 2, CHUNK, 128), F32),
            pltpu.VMEM((CHUNK, WIDTH), F32),
            pltpu.VMEM((2, CHUNK, WIDTH), F32),
            pltpu.VMEM((2, 3, CHUNK, WIDTH), BF16),
            pltpu.VMEM((2, 3, CHUNK, WIDTH), BF16),
            pltpu.VMEM((2, 4, 64, WIDTH), F32),
            pltpu.VMEM((2, 3, 64, WIDTH), BF16),
            pltpu.VMEM((2, 3, 64, WIDTH), BF16),
            pltpu.VMEM((2, 4, ROWS, WIDTH), F32),
            pltpu.VMEM((2, 3, ROWS, WIDTH), F32),
            pltpu.VMEM((2, 3, ROWS, WIDTH), F32),
            pltpu.VMEM((2 * ROWS, WIDTH), BF16),
            pltpu.VMEM((2 * ROWS, WIDTH), BF16),
            pltpu.VMEM((1, 128), I32),
            pltpu.VMEM((1, 128), I32),
            dma,
            dma,
            dma((2, 3, 3)), dma((2, 3, 3)), dma((2, 3, 3)), dma((2, 3, 3)),
            dma((3, 3)), dma((3, 3)),
            dma((2, 3, 3)), dma((2, 3, 3)),
            dma((3,)), dma((3,)), dma((2,)), dma((2,)),
        ],
        compiler_params=pltpu.CompilerParams(
            collective_id=0, has_side_effects=True, vmem_limit_bytes=60 * 1024 * 1024
        ),
        name="xbm",
    )(
        step_index,
        batch_rows,
        labels,
        memory_labels.reshape(1, KEYS_DEV),
        keep_bits.reshape(1, KEYS_DEV),
        memory,
    )
    slot = step_index[0] % (memory.shape[0] // local_rows)
    new_memory = lax.dynamic_update_slice_in_dim(kept_memory, moved, slot * local_rows, 0)
    new_labels = lax.dynamic_update_slice_in_dim(
        memory_labels, moved_labels[0, :local_rows], slot * local_rows, 0
    )
    return grad, loss[:, 0], new_memory, new_labels


def solution(mesh):
    rows = P(("grp", "dev"), None)
    flat = P(("grp", "dev"))
    return jax.shard_map(
        per_device,
        mesh=mesh,
        in_specs=(rows, flat, rows, flat, flat, P()),
        out_specs=(rows, flat, rows, flat),
        check_vma=False,
    )
```

time: 901 us -> 96.4 us (0.11)
  waiting for transfers between devices: 653 us -> 0 us
  blocking collectives: 132 us -> 0 us
  Pallas kernels: 0 us -> 83.5 us
  matrix products: 80 us -> 0 us
  other arithmetic: 16.7 us -> 0 us
  between operations: 14.9 us -> 1.31 us
    reduce_scatter x1 -> x0, waiting for transfers between devices: 653 us -> none  [per_device(): lax.psum_scatter(combined, ('grp', 'dev'), scatter_dimension=0, tiled=True)]
    pallas_call x0 -> x1, Pallas kernels: none -> 83.5 us  [per_device(): pl.pallas_call(kernel, out_shape=(jax.ShapeDtypeStruct((local_rows, WIDTH...]
    dot_general x24 -> x0, matrix products: 80 us -> none  [the longest x8 40.9 us: score_block(): lax.dot_general(block_anchors, memory_keys, (((1,), (1,)), ((), ())), pre...]
    unnamed x1 -> x0, blocking collectives: 68.7 us -> none
    psum x1 -> x0, blocking collectives: 63.2 us -> none  [per_device(): pos_total, neg_total = lax.psum((pos_sum, neg_sum), ('grp', 'dev'))]
    sub x1 -> x0, other arithmetic: 10.1 us -> none  [per_device(): push / (1.0 + neg_total)[:, None] - pull / (1.0 + pos_total)[:, None]]
  transfers between devices with their start and end apart: 2 -> 0, of which waited for: 1 -> 0; matrix products, arithmetic and copies ran while one was open for 0% -> 0% of each run, Pallas kernels for 0% -> 0%
where the time goes in v1:
time: 96.4 us; the launch traced here: 95.9 us
  Pallas kernels  83.5 us (87%)
  local copies, waits for them, and re-layouts  11.1 us (12%)
  between operations  1.31 us (1%)
    pallas_call x1, Pallas kernels, per_device(): pl.pallas_call(kernel, out_shape=(jax.ShapeDtypeStruct((local_rows, WIDTH...  83.5 us
    unnamed x3, local copies, waits for them, and re-layouts  5.81 us

profile of v1, /device:TPU:0, one launch (start us, length us, event | category | flops | bytes accessed | tf_op | source)
XLA Modules:
  0.0 95.9 jit_solution(5765069420590003096)
XLA Ops:
  0.6 1.3 %copy.16 = s32[2048]{0:T(1024)} copy(s32[2048]{0:T(1024)} %param.9) | data formatting | bytes 16384
  2.6 1.2 %pad_bitcast_fusion.blab_ref = s32[1,128]{1,0:T(1,128)} fusion(s32[32]{0:T(128)} %param.7), kind=kLoop, calls=%fused_computation.2 | loop fusion | bytes 640 | tf_op jit(solution)/shard_map/reshape | solution.py:370
  3.8 83.5 %xbm.1 = (f32[32,512]{1,0:T(8,128)}, f32[32,128]{1,0:T(8,128)}, bf16[32,512]{1,0:T(8,128)(2,1)}, s32[1,128]{1,0:T(1,128)}, bf16[2048,512]{1,0:T(8,128)(2,1)}) custom-call(s32[1]{0:T(128)} %copy.15.step_ref, bf16[32,512]{1,0:T(8,128)(2,1)} %batch_ref.1, s32[1,128]{1,0:T(1,128)} %pad_bitcast_fusion.blab_ref, s32[1,2048]{1,0:T(1,128)} %bitcast.10, ...), custom_call_target="tpu_custom_call" | custom-call | tf_op jit(solution)/shard_map/xbm/pallas_call | solution.py:371
  87.3 1.4 %bitcast_dynamic-update-slice_fusion = s32[2048]{0:T(1024)} fusion(s32[2048]{0:T(1024)} %copy.16, s32[]{:T(128)S(6)} %select_n.12, s32[1,128]{1,0:T(1,128)} %get-tuple-element.13), kind=kLoop, calls=%fused_computation.1 | loop fusion | bytes 1028 | tf_op jit(solution)/shard_map/dynamic_update_slice | solution.py:432
  88.7 1.3 %slice_reduce_fusion = f32[32]{0:T(128)} fusion(f32[32,128]{1,0:T(8,128)} %get-tuple-element.10), kind=kLoop, calls=%fused_computation | loop fusion | bytes 256 | tf_op jit(solution)/shard_map/slice | solution.py:435
  90.0 1.4 %constant_dynamic-update-slice_fusion = bf16[2048,512]{1,0:T(8,128)(2,1)} fusion(bf16[2048,512]{1,0:T(8,128)(2,1)} %get-tuple-element.11, bf16[32,512]{1,0:T(8,128)(2,1)} %get-tuple-element.12, s32[]{:T(128)S(6)} %select_n.12), kind=kLoop, calls=%fused_computation.3 | loop fusion | bytes 65540 | tf_op jit(solution)/shard_map/dynamic_update_slice | solution.py:431
  91.4 1.5 %copy.17 = f32[32,512]{1,0:T(8,128)} copy(f32[32,512]{1,0:T(8,128)} %get-tuple-element.18) | data formatting | bytes 131072
  92.8 3.0 %copy.18 = bf16[2048,512]{1,0:T(8,128)(2,1)} copy(bf16[2048,512]{1,0:T(8,128)(2,1)} %constant_dynamic-update-slice_fusion) | data formatting | bytes 4194304

commit v2 on v1

--- a/solution.py
+++ b/solution.py
@@ -21,8 +21,7 @@
 WIDTH = 512
 KEYS_DEV = 2048
 KEYS = 4096
-S_TILE = 2048
-VISIT = (0, 1, 3, 2)
+SLOTS = KEYS_DEV // (2 * ROWS)
 
 
 def column(row):
@@ -35,10 +34,10 @@
 
 def kernel(
     step_ref, batch_ref, blab_ref, mlab_ref, keep_ref, mem_ref,
-    grad_ref, loss_ref, moved_ref, mvlab_ref, newmem_ref,
+    grad_ref, loss_ref, moved_ref, mvlab_ref,
     mraw, klraw, kpraw, keys, klab, raw, labs, an, labc, terms, acc, sums, sums_in, den,
-    gpart, gown, sb1, rb1, g1, sb2, rb2, g2, sb3, rb3, cand, cand_in, clab, clab_in,
-    mem_sem, out_sem, agd_s, agd_r, agl_s, agl_r, ar_s, ar_r, rs_s, rs_r, pt_s, pt_r, bt_s, bt_r,
+    pair, gown, sb1, rb1, g1, sb2, rb2, g2, sb3, rb3, cand, cand_in, clab, clab_in,
+    mem_sem, agd_s, agd_r, agl_s, agl_r, ar_s, ar_r, rs_s, rs_r, pt_s, pt_r, bt_s, bt_r,
 ):
     n_dev = lax.axis_size("dev")
     me = lax.axis_index("grp") * n_dev + lax.axis_index("dev")
@@ -68,9 +67,11 @@
         for off in (1, 2, 3):
             pl.semaphore_signal(barrier, inc=1, device_id=peer(axis, off), device_id_type=MESH)
     pl.semaphore_signal(barrier, inc=1, device_id=partner, device_id_type=MESH)
+    for i in range(4):
+        clab[:, 2 * ROWS * i : 2 * ROWS * (i + 1)] = blab_ref[...]
     for p, (f, m, l) in enumerate(ORDERS):
         raw[p, at[l], at[m], at[f]] = batch_ref[pl.ds(p * ROWS, ROWS), :]
-        labs[p, at[l], at[m], at[f]] = blab_ref[...]
+        labs[p, at[l], at[m], at[f]] = clab[...]
     pl.semaphore_wait(barrier, 10)
 
     def slot(ref, p, phase, off):
@@ -118,7 +119,7 @@
         def block(i, _):
             row = pl.multiple_of(i * 128, 128)
             kept = kpraw[half, :, pl.ds(row, 128)] > 0
-            klab[half, :, pl.ds(row, 128)] = jnp.where(
+            klab[:, pl.ds(pl.multiple_of(half * KEYS_DEV + row, 128), 128)] = jnp.where(
                 kept, klraw[half, :, pl.ds(row, 128)], -1
             ).astype(F32)
             values = mraw[half, pl.ds(row, 128), :].astype(F32)
@@ -129,8 +130,6 @@
         lax.fori_loop(0, KEYS_DEV // 128, block, 0)
 
     own_mem.wait()
-    out_mem = pltpu.make_async_copy(mraw.at[0], newmem_ref, out_sem)
-    out_mem.start()
     normalize_memory(0)
     gather_recv(0)
     gather_start(1)
@@ -149,70 +148,84 @@
         an[p, l] = (values * unit_scale(values)).astype(BF16)
         pages = labs[p, l].reshape(16, 128).astype(F32)
         wide = jnp.transpose(jnp.concatenate([pages] * 8, axis=0))
+        mine = jnp.where(jnp.full((ROWS, 128), p, I32) == 0, wide[:ROWS], wide[ROWS : 2 * ROWS])
         for b in range(16):
-            labc[p, l, pl.ds(b * ROWS, ROWS), :] = jnp.broadcast_to(
-                wide[p * ROWS : (p + 1) * ROWS, b : b + 1], (ROWS, 128)
-            )
+            labc[p, l, pl.ds(b * ROWS, ROWS), :] = jnp.broadcast_to(mine[:, b : b + 1], (ROWS, 128))
 
     def score(p, l):
-        acc[...] = jnp.zeros_like(acc)
-
-        def tile(t, _):
-            first = pl.multiple_of(t * S_TILE, S_TILE)
-            s = lax.dot_general(
-                an[p, l], keys[pl.ds(first, S_TILE), :], (((1,), (1,)), ((), ())),
-                preferred_element_type=F32,
-            )
-            labels = labc[p, l]
-            all_sum, pos_sum = acc[0], acc[1]
-            for j in range(S_TILE // 128):
-                sj = s[:, j * 128 : (j + 1) * 128]
-                same = labels == klab[t, :, j * 128 : (j + 1) * 128]
-                e = jnp.exp2(sj * jnp.where(same, -2.0 * LOG2E, 50.0 * LOG2E))
-                all_sum = all_sum + e
-                pos_sum = pos_sum + jnp.where(same, e, 0.0)
-                terms[p, l, :, pl.ds(pl.multiple_of(first + j * 128, 128), 128)] = e.astype(BF16)
-            acc[0], acc[1] = all_sum, pos_sum
-            return 0
-
-        lax.fori_loop(0, KEYS // S_TILE, tile, 0)
+        s = lax.dot_general(
+            an[p, l], keys[...], (((1,), (1,)), ((), ())), preferred_element_type=F32
+        )
+        labels = labc[p, l]
+        all_sum = jnp.zeros((CHUNK, 128), F32)
+        pos_sum = jnp.zeros((CHUNK, 128), F32)
+        for j in range(0, KEYS, 128):
+            same = labels == klab[:, j : j + 128]
+            e = jnp.exp2(s[:, j : j + 128] * jnp.where(same, -2.0 * LOG2E, 50.0 * LOG2E))
+            all_sum = all_sum + e
+            pos_sum = pos_sum + jnp.where(same, e, 0.0)
+            terms[p, l, :, j : j + 128] = e.astype(BF16)
+        acc[0], acc[1] = all_sum, pos_sum
         for h in (0, 1):
             half = pl.ds(h * 128, 128)
             total = jnp.sum(jnp.transpose(acc[0, half, :]), axis=0, keepdims=True)
             pos = jnp.sum(jnp.transpose(acc[1, half, :]), axis=0, keepdims=True)
-            sums[0, p, l, h : h + 1, :] = total - pos - dropped
-            sums[0, p, l, 2 + h : 3 + h, :] = pos
+            sums[0, p, l, pl.ds(h, 1), :] = total - pos - dropped
+            sums[0, p, l, pl.ds(2 + h, 1), :] = pos
+
+    def last(p):
+        return jnp.where(p == 0, at[2], at[1])
+
+    def last_peer(p, off):
+        there = (last(p) + off) % 4
+        return device(me + (there - last(p)) * jnp.where(p == 0, 2 * STRIDES[2], 2 * STRIDES[1]))
 
     def visit(i, _):
-        off = jnp.where(i == 2, 3, jnp.where(i == 3, 2, i))
-        for p in (0, 1):
-            f, m, l = (at[a] for a in ORDERS[p])
-            here = (l + 4 - off) % 4
-
-            @pl.when(off > 0)
-            def _():
-                to = peer(ORDERS[p][2], 1)
-                k = jnp.maximum(off - 1, 0)
-                rows, labels = raw.at[p, here], labs.at[p, here]
-                remote(rows, rows, agd_s.at[p, 2, k], agd_r.at[p, 2, k], to).wait_recv()
-                remote(labels, labels, agl_s.at[p, 2, k], agl_r.at[p, 2, k], to).wait_recv()
-
-            prepare(p, here)
-            score(p, here)
+        p, turn = i % 2, i // 2
+        off = jnp.where(turn == 2, 3, jnp.where(turn == 3, 2, turn))
+        here = (last(p) + 4 - off) % 4
+
+        @pl.when(turn > 0)
+        def _():
+            k = jnp.maximum(off - 1, 0)
+            rows, labels = raw.at[p, here], labs.at[p, here]
+            remote(rows, rows, agd_s.at[p, 2, k], agd_r.at[p, 2, k], partner).wait_recv()
+            remote(labels, labels, agl_s.at[p, 2, k], agl_r.at[p, 2, k], partner).wait_recv()
+
+        prepare(p, here)
+        score(p, here)
         return 0
 
-    lax.fori_loop(0, 4, visit, 0)
-
-    for phase in range(3):
+    lax.fori_loop(0, 8, visit, 0)
+
+    def part(p, l, weight):
+        labels = labc[p, l]
+        parts = []
+        for j in range(0, KEYS, 128):
+            same = labels == klab[:, j : j + 128]
+            parts.append(weight(same, terms[p, l, :, j : j + 128].astype(F32)).astype(BF16))
+        return jnp.dot(jnp.concatenate(parts, axis=1), keys[...], preferred_element_type=F32)
+
+    def early(i):
+        return i % 2, jnp.where(i == 2, 1, 2)
+
+    def add_up(phase, _):
+        coord = jnp.where(phase == 0, at[0], jnp.where(phase == 1, at[1], at[2]))
+        stride = jnp.where(phase == 0, 2 * STRIDES[0], jnp.where(phase == 1, 2 * STRIDES[1], 2 * STRIDES[2]))
         copies = [
             remote(
                 sums.at[phase], sums_in.at[phase, off - 1],
-                ar_s.at[phase, off - 1], ar_r.at[phase, off - 1], peer(phase, off),
+                ar_s.at[phase, off - 1], ar_r.at[phase, off - 1],
+                device(me + ((coord + off) % 4 - coord) * stride),
             )
             for off in (1, 2, 3)
         ]
         for copy in copies:
             copy.start()
+        p, off = early(phase)
+        l = (last(p) + off) % 4
+        pair[0, phase] = part(p, l, lambda same, e: jnp.where(same, 0.0, e))
+        pair[1, phase] = part(p, l, lambda same, e: jnp.where(same, e, 0.0))
         for copy in copies:
             copy.wait_recv()
         sums[phase + 1] = (
@@ -220,51 +233,51 @@
         )
         for copy in copies:
             copy.wait_send()
+        return 0
+
+    lax.fori_loop(0, 3, add_up, 0)
 
     def ring1(p, off):
-        k = off - 1
+        k = jnp.maximum(off - 1, 0)
         return remote(
-            sb1.at[p, k], rb1.at[p, k], rs_s.at[p, 0, k], rs_r.at[p, 0, k], peer(ORDERS[p][2], off)
-        )
-
-    def grads(p, l):
+            sb1.at[p, k], rb1.at[p, k], rs_s.at[p, 0, k], rs_r.at[p, 0, k], last_peer(p, off)
+        )
+
+    def weights(p, l):
         for h in (0, 1):
             half = pl.ds(h * 128, 128)
-            den[p, l, 0, half, :] = column(1.0 + EXP_NEG * sums[3, p, l, h : h + 1, :])
-            den[p, l, 1, half, :] = column(1.0 + EXP_POS * sums[3, p, l, 2 + h : 3 + h, :])
-        gpart[...] = jnp.zeros_like(gpart)
-        labels = labc[p, l]
-        neg = EXP_NEG / den[p, l, 0]
-        pos = -EXP_POS / den[p, l, 1]
-
-        def tile(t, _):
-            first = pl.multiple_of(t * S_TILE, S_TILE)
-            parts = []
-            for j in range(S_TILE // 128):
-                e = terms[p, l, :, pl.ds(pl.multiple_of(first + j * 128, 128), 128)].astype(F32)
-                same = labels == klab[t, :, j * 128 : (j + 1) * 128]
-                parts.append((e * jnp.where(same, pos, neg)).astype(BF16))
-            gpart[...] += jnp.dot(
-                jnp.concatenate(parts, axis=1), keys[pl.ds(first, S_TILE), :],
-                preferred_element_type=F32,
-            )
-            return 0
-
-        lax.fori_loop(0, KEYS // S_TILE, tile, 0)
+            den[p, l, 0, half, :] = column(1.0 + EXP_NEG * sums[3, p, l, pl.ds(h, 1), :])
+            den[p, l, 1, half, :] = column(1.0 + EXP_POS * sums[3, p, l, pl.ds(2 + h, 1), :])
+        return EXP_NEG / den[p, l, 0], -EXP_POS / den[p, l, 1]
+
+    def push_early(i, _):
+        p, off = early(i)
+        neg, pos = weights(p, (last(p) + off) % 4)
+        for j in range(0, WIDTH, 128):
+            some = pl.ds(j, 128)
+            sb1[p, off - 1, :, some] = (
+                pair[0, i, :, some] * neg + pair[1, i, :, some] * pos
+            ).astype(BF16)
+        ring1(p, off).start()
+        return 0
+
+    lax.fori_loop(0, 3, push_early, 0)
 
     def push(i, _):
-        off = jnp.where(i == 0, 2, jnp.where(i == 1, 1, 3))
-        for p in (0, 1):
-            l = (at[ORDERS[p][2]] + off) % 4
-            grads(p, l)
-            sb1[p, off - 1] = gpart[...].astype(BF16)
+        p, off = (i + 1) % 2, jnp.where(i == 0, 1, jnp.where(i < 3, 3, 0))
+        l = (last(p) + off) % 4
+        neg, pos = weights(p, l)
+        g = part(p, l, lambda same, e: e * jnp.where(same, pos, neg))
+        gown[p] = g
+
+        @pl.when(i < 3)
+        def _():
+            sb1[p, jnp.maximum(off - 1, 0)] = g.astype(BF16)
             ring1(p, off).start()
+
         return 0
 
-    lax.fori_loop(0, 3, push, 0)
-    for p in (0, 1):
-        grads(p, at[ORDERS[p][2]])
-        gown[p] = gpart[...]
+    lax.fori_loop(0, 5, push, 0)
 
     step = step_ref[0]
     odd = step % 2
@@ -351,7 +364,6 @@
     moved_ref[...] = jnp.where(keep_mine, cand[...].astype(F32), cand_in[...].astype(F32)).astype(BF16)
     mvlab_ref[...] = jnp.where(jnp.full((1, 128), odd, I32) == 0, clab[...], clab_in[...])
 
-    out_mem.wait()
     for copy in swaps + trade:
         copy.wait_send()
     for p in (0, 1):
@@ -363,28 +375,67 @@
                 ring(p, off).wait_send()
 
 
+def finish(
+    step_ref, grad_ref, loss_ref, moved_ref, mvlab_ref, mlab_ref, mem_ref,
+    grad_out, loss_out, lab_out, mem_out, buf, sem_in, sem_out,
+):
+    pieces, size = buf.shape[0], buf.shape[1]
+    slot = step_ref[0] % SLOTS
+    loads = [
+        pltpu.make_async_copy(mem_ref.at[pl.ds(i * size, size)], buf.at[i], sem_in.at[i])
+        for i in range(pieces)
+    ]
+    stores = [
+        pltpu.make_async_copy(buf.at[i], mem_out.at[pl.ds(i * size, size)], sem_out.at[i])
+        for i in range(pieces)
+    ]
+    for load in loads:
+        load.start()
+    grad_out[...] = grad_ref[...]
+    rows = loss_ref.shape[0]
+    diagonal = lax.broadcasted_iota(I32, (rows, 128), 0) == lax.broadcasted_iota(I32, (rows, 128), 1)
+    loss_out[...] = jnp.sum(jnp.where(diagonal, loss_ref[...], 0.0), axis=0, keepdims=True)[:, :rows]
+    lane = lax.broadcasted_iota(I32, (1, 128), 1) // (2 * ROWS)
+    for i in range(KEYS_DEV // 128):
+        here = pl.ds(i * 128, 128)
+        lab_out[:, here] = jnp.where(
+            lane + i * (64 // ROWS) == jnp.full((1, 128), slot, I32), mvlab_ref[...], mlab_ref[:, here]
+        )
+    per_piece = size // (2 * ROWS)
+    for i in range(pieces):
+        loads[i].wait()
+
+        @pl.when(slot // per_piece == i)
+        def _():
+            at = pl.multiple_of((slot % per_piece) * (2 * ROWS), 2 * ROWS)
+            buf[i, pl.ds(at, 2 * ROWS), :] = moved_ref[...]
+
+        stores[i].start()
+    for store in stores:
+        store.wait()
+
+
 def per_device(batch_rows, batch_labels, memory, memory_labels, keep_bits, step_index):
     local_rows = batch_rows.shape[0]
     vmem = pl.BlockSpec(memory_space=pltpu.VMEM)
     dma = pltpu.SemaphoreType.DMA
-    labels = jnp.pad(batch_labels, (0, 128 - local_rows)).reshape(1, 128)
-    grad, loss, moved, moved_labels, kept_memory = pl.pallas_call(
+    memory_labels_row = memory_labels.reshape(1, KEYS_DEV)
+    grad, loss, moved, moved_labels = pl.pallas_call(
         kernel,
         out_shape=(
             jax.ShapeDtypeStruct((local_rows, WIDTH), F32),
             jax.ShapeDtypeStruct((local_rows, 128), F32),
             jax.ShapeDtypeStruct((local_rows, WIDTH), BF16),
             jax.ShapeDtypeStruct((1, 128), I32),
-            jax.ShapeDtypeStruct((KEYS_DEV, WIDTH), BF16),
         ),
         in_specs=[pl.BlockSpec(memory_space=pltpu.SMEM), vmem, vmem, vmem, vmem, pl.BlockSpec(memory_space=pl.ANY)],
-        out_specs=(vmem, vmem, vmem, vmem, pl.BlockSpec(memory_space=pl.ANY)),
+        out_specs=(vmem, vmem, vmem, vmem),
         scratch_shapes=[
             pltpu.VMEM((2, KEYS_DEV, WIDTH), BF16),
             pltpu.VMEM((2, 1, KEYS_DEV), I32),
             pltpu.VMEM((2, 1, KEYS_DEV), I32),
             pltpu.VMEM((KEYS, WIDTH), BF16),
-            pltpu.VMEM((2, 1, KEYS_DEV), F32),
+            pltpu.VMEM((1, KEYS), F32),
             pltpu.VMEM((2, 4, 4, 4, ROWS, WIDTH), BF16),
             pltpu.VMEM((2, 4, 4, 4, 1, 128), I32),
             pltpu.VMEM((2, 4, CHUNK, WIDTH), BF16),
@@ -394,7 +445,7 @@
             pltpu.VMEM((4, 2, 4, 4, 128), F32),
             pltpu.VMEM((3, 3, 2, 4, 4, 128), F32),
             pltpu.VMEM((2, 4, 2, CHUNK, 128), F32),
-            pltpu.VMEM((CHUNK, WIDTH), F32),
+            pltpu.VMEM((2, 3, CHUNK, WIDTH), F32),
             pltpu.VMEM((2, CHUNK, WIDTH), F32),
             pltpu.VMEM((2, 3, CHUNK, WIDTH), BF16),
             pltpu.VMEM((2, 3, CHUNK, WIDTH), BF16),
@@ -409,7 +460,6 @@
             pltpu.VMEM((1, 128), I32),
             pltpu.VMEM((1, 128), I32),
             dma,
-            dma,
             dma((2, 3, 3)), dma((2, 3, 3)), dma((2, 3, 3)), dma((2, 3, 3)),
             dma((3, 3)), dma((3, 3)),
             dma((2, 3, 3)), dma((2, 3, 3)),
@@ -422,17 +472,29 @@
     )(
         step_index,
         batch_rows,
-        labels,
-        memory_labels.reshape(1, KEYS_DEV),
+        batch_labels.reshape(1, local_rows),
+        memory_labels_row,
         keep_bits.reshape(1, KEYS_DEV),
         memory,
     )
-    slot = step_index[0] % (memory.shape[0] // local_rows)
-    new_memory = lax.dynamic_update_slice_in_dim(kept_memory, moved, slot * local_rows, 0)
-    new_labels = lax.dynamic_update_slice_in_dim(
-        memory_labels, moved_labels[0, :local_rows], slot * local_rows, 0
-    )
-    return grad, loss[:, 0], new_memory, new_labels
+    smem, hbm = pl.BlockSpec(memory_space=pltpu.SMEM), pl.BlockSpec(memory_space=pl.ANY)
+    pieces = 4
+    grad, loss_row, new_labels, new_memory = pl.pallas_call(
+        finish,
+        out_shape=(
+            jax.ShapeDtypeStruct((local_rows, WIDTH), F32),
+            jax.ShapeDtypeStruct((1, local_rows), F32),
+            jax.ShapeDtypeStruct((1, KEYS_DEV), I32),
+            jax.ShapeDtypeStruct((KEYS_DEV, WIDTH), BF16),
+        ),
+        in_specs=[smem, vmem, vmem, vmem, vmem, vmem, hbm],
+        out_specs=(vmem, vmem, vmem, hbm),
+        scratch_shapes=[
+            pltpu.VMEM((pieces, KEYS_DEV // pieces, WIDTH), BF16), dma((pieces,)), dma((pieces,)),
+        ],
+        name="finish",
+    )(step_index, grad, loss, moved, moved_labels, memory_labels_row, memory)
+    return grad, loss_row.reshape(local_rows), new_memory, new_labels.reshape(KEYS_DEV)
 
 
 def solution(mesh):

time: 96.4 us -> 78.9 us (0.82)
  local copies, waits for them, and re-layouts: 11.1 us -> 0 us
  Pallas kernels: 83.5 us -> 77.3 us
    pallas_call x1, Pallas kernels: 83.5 us -> 73.4 us  [per_device(): pl.pallas_call(kernel, out_shape=(jax.ShapeDtypeStruct((local_rows, WIDTH...]
    unnamed x3 -> x0, local copies, waits for them, and re-layouts: 5.81 us -> none
    pallas_call x0 -> x1, Pallas kernels: none -> 3.93 us  [per_device(): pl.pallas_call(finish, out_shape=(jax.ShapeDtypeStruct((local_rows, WIDTH...]
    dynamic_update_slice x2 -> x0, local copies, waits for them, and re-layouts: 2.74 us -> none  [the longest x1 1.38 us: per_device(): lax.dynamic_update_slice_in_dim(memory_labels, moved_labels[0, :local_row...]
    slice x1 -> x0, local copies, waits for them, and re-layouts: 1.34 us -> none  [per_device(): return (grad, loss[:, 0], new_memory, new_labels)]
    reshape x1 -> x0, local copies, waits for them, and re-layouts: 1.17 us -> none  [per_device(): labels = jnp.pad(batch_labels, (0, 128 - local_rows)).reshape(1, 128)]
where the time goes in v2:
time: 78.9 us; the launch traced here: 78.6 us
  Pallas kernels  77.3 us (98%)
  between operations  1.29 us (2%)
    pallas_call x1, Pallas kernels, per_device(): pl.pallas_call(kernel, out_shape=(jax.ShapeDtypeStruct((local_rows, WIDTH...  73.4 us
    pallas_call x1, Pallas kernels, per_device(): pl.pallas_call(finish, out_shape=(jax.ShapeDtypeStruct((local_rows, WIDTH...  3.93 us

profile of v2, /device:TPU:0, one launch (start us, length us, event | category | flops | bytes accessed | tf_op | source)
XLA Modules:
  0.0 78.6 jit_solution(7793244811539126668)
XLA Ops:
  1.3 73.4 %xbm.1 = (f32[32,512]{1,0:T(8,128)}, f32[32,128]{1,0:T(8,128)}, bf16[32,512]{1,0:T(8,128)(2,1)}, s32[1,128]{1,0:T(1,128)}) custom-call(s32[1]{0:T(128)S(6)} %copy.10.step_ref, bf16[32,512]{1,0:T(8,128)(2,1)} %batch_ref.1, s32[1,32]{1,0:T(1,128)} %bitcast.8, s32[1,2048]{1,0:T(1,128)} %bitcast.5, s32[1,2048]{1,0:T(1,128)} %bitcast.7, bf16[2048,512]{1,0:T(8,128)(2,1)} %mem_ref.3), custom_call_target="tpu_custom_call" | custom-call | tf_op jit(solution)/shard_map/xbm/pallas_call | solution.py:423
  74.7 3.9 %finish.1 = (f32[32,512]{1,0:T(8,128)}, f32[1,32]{1,0:T(1,128)}, s32[1,2048]{1,0:T(1,128)}, bf16[2048,512]{1,0:T(8,128)(2,1)}) custom-call(s32[1]{0:T(128)S(6)} %copy.10.step_ref, f32[32,512]{1,0:T(8,128)} %get-tuple-element.12.grad_ref, f32[32,128]{1,0:T(8,128)} %get-tuple-element.13.loss_ref, bf16[32,512]{1,0:T(8,128)(2,1)} %get-tuple-element.14.moved_ref, ...), custom_call_target="tpu_custom_call" | custom-call | tf_op jit(solution)/shard_map/finish/pallas_call | solution.py:482

commit v3 on v2

--- a/solution.py
+++ b/solution.py
@@ -14,8 +14,6 @@
 EXP_NEG = math.exp(-25.0)
 EXP_POS = math.exp(1.0)
 
-ORDERS = ((0, 1, 2), (2, 0, 1))
-STRIDES = (16, 4, 1)
 ROWS = 16
 CHUNK = 256
 WIDTH = 512
@@ -35,9 +33,10 @@
 def kernel(
     step_ref, batch_ref, blab_ref, mlab_ref, keep_ref, mem_ref,
     grad_ref, loss_ref, moved_ref, mvlab_ref,
-    mraw, klraw, kpraw, keys, klab, raw, labs, an, labc, terms, acc, sums, sums_in, den,
-    pair, gown, sb1, rb1, g1, sb2, rb2, g2, sb3, rb3, cand, cand_in, clab, clab_in,
-    mem_sem, agd_s, agd_r, agl_s, agl_r, ar_s, ar_r, rs_s, rs_r, pt_s, pt_r, bt_s, bt_r,
+    mraw, klraw, kpraw, keys, klab, raw, labs, an, labc, terms, acc, sums, sums_in, sums_z, den,
+    pair, gown, sb1, rb1, hb, gr, g1, sb2, rb2, cand, cand_in, clab, clab_in,
+    mem_sem, pl_s, pl_r, pll_s, pll_r, ln_s, ln_r, lnl_s, lnl_r, fw_s, fw_r,
+    as_s, as_r, az_s, az_r, h1_s, h1_r, r1_s, r1_r, r2_s, r2_r, pt_s, pt_r, bt_s, bt_r,
 ):
     n_dev = lax.axis_size("dev")
     me = lax.axis_index("grp") * n_dev + lax.axis_index("dev")
@@ -48,9 +47,22 @@
     def device(index):
         return (index // n_dev, index % n_dev)
 
-    def peer(axis, off):
-        there = (at[axis] + off) % 4
-        return device(me + (there - at[axis]) * (2 * STRIDES[axis]))
+    def chip_at(dx, dy, dz):
+        there = ((at[0] + dx) % 4) * 16 + ((at[1] + dy) % 4) * 4 + (at[2] + dz) % 4
+        return device(2 * there + core)
+
+    def peer(p, dl, dm, df):
+        first, even = p == 0, core == 0
+        dx = jnp.where(first, df, jnp.where(even, dm, dl))
+        dy = jnp.where(first, dm, jnp.where(even, dl, dm))
+        dz = jnp.where(first, dl, df)
+        return chip_at(dx, dy, dz)
+
+    def place(p):
+        first, even = p == 0, core == 0
+        last = jnp.where(first, at[2], jnp.where(even, at[1], at[0]))
+        middle = jnp.where(first, at[1], jnp.where(even, at[0], at[1]))
+        return last, middle, jnp.where(first, at[0], at[2])
 
     partner = device(me + 1 - 2 * core)
 
@@ -63,47 +75,80 @@
     own_mem.start()
 
     barrier = pltpu.get_barrier_semaphore()
-    for axis in range(3):
-        for off in (1, 2, 3):
-            pl.semaphore_signal(barrier, inc=1, device_id=peer(axis, off), device_id_type=MESH)
+    def greet(p, dl, dm, df):
+        pl.semaphore_signal(barrier, inc=1, device_id=peer(p, dl, dm, df), device_id_type=MESH)
+
+    def greet_plane(j, _):
+        greet(0, 0, j // 4, j % 4)
+        return 0
+
+    def greet_diagonal(j, _):
+        greet(1, 0, 1 + j // 3, 1 + j % 3)
+        return 0
+
+    lax.fori_loop(1, 16, greet_plane, 0)
+    lax.fori_loop(0, 9, greet_diagonal, 0)
+    for off in (1, 2, 3):
+        greet(0, off, 0, 0)
     pl.semaphore_signal(barrier, inc=1, device_id=partner, device_id_type=MESH)
     for i in range(4):
         clab[:, 2 * ROWS * i : 2 * ROWS * (i + 1)] = blab_ref[...]
-    for p, (f, m, l) in enumerate(ORDERS):
-        raw[p, at[l], at[m], at[f]] = batch_ref[pl.ds(p * ROWS, ROWS), :]
-        labs[p, at[l], at[m], at[f]] = clab[...]
-    pl.semaphore_wait(barrier, 10)
-
-    def slot(ref, p, phase, off):
-        f, m, l = (at[a] for a in ORDERS[p])
-        if phase == 0:
-            return ref.at[p, l, m, (f + off) % 4]
-        if phase == 1:
-            return ref.at[p, l, (m + off) % 4]
-        return ref.at[p, (l + off) % 4]
-
-    def gather(p, phase, off, back):
-        shift = 4 - off if back else 0
-        to = peer(ORDERS[p][phase], off)
-        rows, labels = slot(raw, p, phase, shift), slot(labs, p, phase, shift)
+    for p in (0, 1):
+        l, m, f = place(p)
+        raw[p, l, m, f] = batch_ref[pl.ds(p * ROWS, ROWS), :]
+        labs[p, l, m, f] = clab[...]
+    pl.semaphore_wait(barrier, 28)
+
+    def to_plane(p, j, back):
+        l, m, f = place(p)
+        dm, df = j // 4, j % 4
+        if back:
+            m, f = (m + 4 - dm) % 4, (f + 4 - df) % 4
+        rows, labels, to = raw.at[p, l, m, f], labs.at[p, l, m, f], peer(p, 0, dm, df)
         return (
-            remote(rows, rows, agd_s.at[p, phase, off - 1], agd_r.at[p, phase, off - 1], to),
-            remote(labels, labels, agl_s.at[p, phase, off - 1], agl_r.at[p, phase, off - 1], to),
-        )
-
-    def gather_start(phase):
-        for off in (1, 3, 2):
-            for p in (0, 1):
-                for copy in gather(p, phase, off, False):
-                    copy.start()
-
-    def gather_recv(phase):
+            remote(rows, rows, pl_s.at[p, j - 1], pl_r.at[p, j - 1], to),
+            remote(labels, labels, pll_s.at[p, j - 1], pll_r.at[p, j - 1], to),
+        )
+
+    def plane_start(j, _):
         for p in (0, 1):
-            for off in (1, 2, 3):
-                for copy in gather(p, phase, off, True):
-                    copy.wait_recv()
-
-    gather_start(0)
+            for copy in to_plane(p, j, False):
+                copy.start()
+        return 0
+
+    def plane_recv(j, _):
+        for p in (0, 1):
+            for copy in to_plane(p, j, True):
+                copy.wait_recv()
+        return 0
+
+    def plane_sent(j, _):
+        for p in (0, 1):
+            for copy in to_plane(p, j, False):
+                copy.wait_send()
+        return 0
+
+    def line_rows(p, off, back):
+        l = place(p)[0]
+        if back:
+            l = (l + 4 - off) % 4
+        rows = raw.at[p, l]
+        return remote(rows, rows, ln_s.at[p, off // 2], ln_r.at[p, off // 2], peer(p, off, 0, 0))
+
+    def line_labels(p, off, back):
+        l = place(p)[0]
+        if back:
+            l = (l + 4 - off) % 4
+        labels = labs.at[p, l]
+        return remote(labels, labels, lnl_s.at[p, off - 1], lnl_r.at[p, off - 1], peer(p, off, 0, 0))
+
+    def relay(p, off, back):
+        l = place(p)[0]
+        l = (l + (2 if back else 4 - off)) % 4
+        half = raw.at[p, l, pl.ds(0 if off == 1 else 2, 2)]
+        return remote(half, half, fw_s.at[p, off // 2], fw_r.at[p, off // 2], peer(p, off, 0, 0))
+
+    lax.fori_loop(1, 16, plane_start, 0)
     swaps = (
         remote(mem_ref, mraw.at[1], pt_s.at[0], pt_r.at[0], partner),
         remote(mlab_ref, klraw.at[1], pt_s.at[1], pt_r.at[1], partner),
@@ -131,13 +176,15 @@
 
     own_mem.wait()
     normalize_memory(0)
-    gather_recv(0)
-    gather_start(1)
+    lax.fori_loop(1, 16, plane_recv, 0)
+    for p in (1, 0):
+        for off in (1, 3):
+            line_rows(p, off, False).start()
+        for off in (1, 3, 2):
+            line_labels(p, off, False).start()
     for copy in swaps:
         copy.wait_recv()
     normalize_memory(1)
-    gather_recv(1)
-    gather_start(2)
 
     dropped = float(KEYS) - jnp.sum(
         jnp.where(kpraw[...] > 0, 1.0, 0.0).reshape(2, KEYS_DEV), axis=(0, 1), keepdims=True
@@ -173,24 +220,24 @@
             sums[0, p, l, pl.ds(h, 1), :] = total - pos - dropped
             sums[0, p, l, pl.ds(2 + h, 1), :] = pos
 
-    def last(p):
-        return jnp.where(p == 0, at[2], at[1])
-
-    def last_peer(p, off):
-        there = (last(p) + off) % 4
-        return device(me + (there - last(p)) * jnp.where(p == 0, 2 * STRIDES[2], 2 * STRIDES[1]))
-
     def visit(i, _):
-        p, turn = i % 2, i // 2
-        off = jnp.where(turn == 2, 3, jnp.where(turn == 3, 2, turn))
-        here = (last(p) + 4 - off) % 4
-
-        @pl.when(turn > 0)
-        def _():
-            k = jnp.maximum(off - 1, 0)
-            rows, labels = raw.at[p, here], labs.at[p, here]
-            remote(rows, rows, agd_s.at[p, 2, k], agd_r.at[p, 2, k], partner).wait_recv()
-            remote(labels, labels, agl_s.at[p, 2, k], agl_r.at[p, 2, k], partner).wait_recv()
+        early_piece = jnp.logical_or(jnp.logical_or(i == 1, i == 2), jnp.logical_or(i == 3, i == 6))
+        p = jnp.where(early_piece, 1, 0)
+        off = jnp.where(i < 2, 0, jnp.where(i > 5, 2, jnp.where(i % 2 == 0, 1, 3)))
+        here = (place(p)[0] + 4 - off) % 4
+
+        @pl.when(jnp.logical_or(i == 2, i == 4))
+        def _():
+            for off in (1, 3):
+                line_rows(p, off, True).wait_recv()
+                relay(p, off, False).start()
+                line_labels(p, off, True).wait_recv()
+
+        @pl.when(i > 5)
+        def _():
+            for off in (1, 3):
+                relay(p, off, True).wait_recv()
+            line_labels(p, 2, True).wait_recv()
 
         prepare(p, here)
         score(p, here)
@@ -209,75 +256,156 @@
     def early(i):
         return i % 2, jnp.where(i == 2, 1, 2)
 
-    def add_up(phase, _):
-        coord = jnp.where(phase == 0, at[0], jnp.where(phase == 1, at[1], at[2]))
-        stride = jnp.where(phase == 0, 2 * STRIDES[0], jnp.where(phase == 1, 2 * STRIDES[1], 2 * STRIDES[2]))
-        copies = [
-            remote(
-                sums.at[phase], sums_in.at[phase, off - 1],
-                ar_s.at[phase, off - 1], ar_r.at[phase, off - 1],
-                device(me + ((coord + off) % 4 - coord) * stride),
-            )
-            for off in (1, 2, 3)
-        ]
-        for copy in copies:
-            copy.start()
-        p, off = early(phase)
-        l = (last(p) + off) % 4
-        pair[0, phase] = part(p, l, lambda same, e: jnp.where(same, 0.0, e))
-        pair[1, phase] = part(p, l, lambda same, e: jnp.where(same, e, 0.0))
-        for copy in copies:
-            copy.wait_recv()
-        sums[phase + 1] = (
-            sums[phase] + sums_in[phase, 0] + sums_in[phase, 1] + sums_in[phase, 2]
-        )
-        for copy in copies:
-            copy.wait_send()
+    def alone(i):
+        p, off = early(i)
+        l = (place(p)[0] + off) % 4
+        pair[0, i] = part(p, l, lambda same, e: jnp.where(same, 0.0, e))
+        pair[1, i] = part(p, l, lambda same, e: jnp.where(same, e, 0.0))
+
+    def sums_plane(j):
+        return remote(
+            sums.at[0], sums_in.at[j - 1], as_s.at[j - 1], as_r.at[j - 1], chip_at(j % 4, j // 4, 0)
+        )
+
+    def sums_line(off):
+        return remote(
+            sums.at[1], sums_z.at[off - 1], az_s.at[off - 1], az_r.at[off - 1], chip_at(0, 0, off)
+        )
+
+    def add_up(i, _):
+        @pl.when(i == 0)
+        def _():
+            def begin(j, _):
+                sums_plane(j).start()
+                return 0
+
+            lax.fori_loop(1, 16, begin, 0)
+
+        alone(i)
+
+        @pl.when(i == 1)
+        def _():
+            def arrive(j, _):
+                sums_plane(j).wait_recv()
+                return 0
+
+            lax.fori_loop(1, 16, arrive, 0)
+            total = sums[0]
+            for j in range(15):
+                total = total + sums_in[j]
+            sums[1] = total
+            for off in (1, 3, 2):
+                sums_line(off).start()
+
         return 0
 
     lax.fori_loop(0, 3, add_up, 0)
-
-    def ring1(p, off):
-        k = jnp.maximum(off - 1, 0)
+    for off in (1, 2, 3):
+        sums_line(off).wait_recv()
+    sums[2] = sums[1] + sums_z[0] + sums_z[1] + sums_z[2]
+
+    def onward(p, off):
+        side = off // 2
         return remote(
-            sb1.at[p, k], rb1.at[p, k], rs_s.at[p, 0, k], rs_r.at[p, 0, k], last_peer(p, off)
-        )
+            sb1.at[p, 2, side], hb.at[p, side], h1_s.at[p, side], h1_r.at[p, side], peer(p, off, 0, 0)
+        )
+
+    def ring1(p, off, half):
+        side = off // 2
+        return remote(
+            sb1.at[p, side, half], rb1.at[p, side, half],
+            r1_s.at[p, side, half], r1_r.at[p, side, half], peer(p, off, 0, 0),
+        )
+
+    def dispatch(p, off, g):
+        side = off // 2
+        gr[p, side] = jnp.where(jnp.full((128, WIDTH), side, I32) == 0, g[:128], g[128:])
+        sb1[p, side, 1 - side] = jnp.where(
+            jnp.full((128, WIDTH), side, I32) == 0, g[128:], g[:128]
+        ).astype(BF16)
+        ring1(p, off, 1 - side).start()
+
+    def complete(p, off):
+        side = off // 2
+        onward(p, off).wait_recv()
+        sb1[p, side, side] = (gr[p, side] + hb[p, side].astype(F32)).astype(BF16)
+        ring1(p, off, side).start()
 
     def weights(p, l):
         for h in (0, 1):
             half = pl.ds(h * 128, 128)
-            den[p, l, 0, half, :] = column(1.0 + EXP_NEG * sums[3, p, l, pl.ds(h, 1), :])
-            den[p, l, 1, half, :] = column(1.0 + EXP_POS * sums[3, p, l, pl.ds(2 + h, 1), :])
+            den[p, l, 0, half, :] = column(1.0 + EXP_NEG * sums[2, p, l, pl.ds(h, 1), :])
+            den[p, l, 1, half, :] = column(1.0 + EXP_POS * sums[2, p, l, pl.ds(2 + h, 1), :])
         return EXP_NEG / den[p, l, 0], -EXP_POS / den[p, l, 1]
 
-    def push_early(i, _):
+    def ready(i):
         p, off = early(i)
-        neg, pos = weights(p, (last(p) + off) % 4)
-        for j in range(0, WIDTH, 128):
-            some = pl.ds(j, 128)
-            sb1[p, off - 1, :, some] = (
-                pair[0, i, :, some] * neg + pair[1, i, :, some] * pos
-            ).astype(BF16)
-        ring1(p, off).start()
-        return 0
-
-    lax.fori_loop(0, 3, push_early, 0)
+        neg, pos = weights(p, (place(p)[0] + off) % 4)
+        return jnp.concatenate(
+            [
+                pair[0, i, :, j : j + 128] * neg + pair[1, i, :, j : j + 128] * pos
+                for j in range(0, WIDTH, 128)
+            ],
+            axis=1,
+        )
+
+    def push_early(p, _):
+        sb1[p, 2] = ready(p).astype(BF16).reshape(2, 128, WIDTH)
+        for off in (1, 3):
+            onward(p, off).start()
+        return 0
+
+    lax.fori_loop(0, 2, push_early, 0)
+    dispatch(0, 1, ready(2))
 
     def push(i, _):
         p, off = (i + 1) % 2, jnp.where(i == 0, 1, jnp.where(i < 3, 3, 0))
-        l = (last(p) + off) % 4
+        l = (place(p)[0] + off) % 4
         neg, pos = weights(p, l)
-        g = part(p, l, lambda same, e: e * jnp.where(same, pos, neg))
-        gown[p] = g
-
-        @pl.when(i < 3)
-        def _():
-            sb1[p, jnp.maximum(off - 1, 0)] = g.astype(BF16)
-            ring1(p, off).start()
+        gown[p] = part(p, l, lambda same, e: e * jnp.where(same, pos, neg))
+
+        @pl.when(i == 0)
+        def _():
+            dispatch(1, 1, gown[1])
+
+        @pl.when(i == 1)
+        def _():
+            dispatch(0, 3, gown[0])
+            complete(1, 1)
+
+        @pl.when(i == 2)
+        def _():
+            dispatch(1, 3, gown[1])
+            complete(0, 1)
+            complete(0, 3)
+            complete(1, 3)
 
         return 0
 
     lax.fori_loop(0, 5, push, 0)
+
+    def ring2(p, j):
+        l, m, f = place(p)
+        dm, df = j // 4, j % 4
+        block = ((m + dm) % 4) * 4 + (f + df) % 4
+        return remote(
+            sb2.at[p, block], rb2.at[p, j - 1], r2_s.at[p, j - 1], r2_r.at[p, j - 1], peer(p, 0, dm, df)
+        )
+
+    for p in (0, 1):
+        for off in (1, 3):
+            for half in (0, 1):
+                ring1(p, off, half).wait_recv()
+        g1[p] = (
+            gown[p].reshape(2, 128, WIDTH) + rb1[p, 0].astype(F32) + rb1[p, 1].astype(F32)
+        ).reshape(16, ROWS, WIDTH)
+        sb2[p] = g1[p].astype(BF16)
+
+        def begin(j, _):
+            ring2(p, j).start()
+            return 0
+
+        lax.fori_loop(1, 16, begin, 0)
 
     step = step_ref[0]
     odd = step % 2
@@ -291,7 +419,8 @@
         qx, qy, qz = q // 16, (q // 4) % 4, q % 4
         pick = wanted == q
         upper = an[0, qz, pl.ds(pl.multiple_of((qy * 4 + qx) * ROWS, ROWS), ROWS), :].astype(F32)
-        lower = an[1, qy, pl.ds(pl.multiple_of((qx * 4 + qz) * ROWS, ROWS), ROWS), :].astype(F32)
+        ql, qm = jnp.where(core == 0, qy, qx), jnp.where(core == 0, qx, qy)
+        lower = an[1, ql, pl.ds(pl.multiple_of((qm * 4 + qz) * ROWS, ROWS), ROWS), :].astype(F32)
         return (
             jnp.where(pick, upper, found[0]),
             jnp.where(pick, lower, found[1]),
@@ -312,51 +441,27 @@
     for copy in trade:
         copy.start()
 
-    def ring2(p, off):
-        return remote(
-            sb2.at[p, off - 1], rb2.at[p, off - 1], rs_s.at[p, 1, off - 1], rs_r.at[p, 1, off - 1],
-            peer(ORDERS[p][1], off),
-        )
-
-    def ring3(p, off):
-        return remote(
-            sb3.at[p, off - 1], rb3.at[p, off - 1], rs_s.at[p, 2, off - 1], rs_r.at[p, 2, off - 1],
-            peer(ORDERS[p][0], off),
-        )
-
     for p in (0, 1):
-        m = at[ORDERS[p][1]]
-        for off in (1, 2, 3):
-            ring1(p, off).wait_recv()
-        g1[p] = (
-            gown[p] + rb1[p, 0].astype(F32) + rb1[p, 1].astype(F32) + rb1[p, 2].astype(F32)
-        ).reshape(4, 64, WIDTH)
-        for off in (1, 2, 3):
-            sb2[p, off - 1] = g1[p, (m + off) % 4].astype(BF16)
-            ring2(p, off).start()
+        l, m, f = place(p)
+        own = pl.ds(pl.multiple_of((m * 4 + f) * ROWS, ROWS), ROWS)
+        mine = pl.ds(p * ROWS, ROWS)
+        loss_ref[mine, :] = jnp.log(den[p, l, 1, own, :]) / 2.0 + jnp.log(den[p, l, 0, own, :]) / 50.0
     for p in (0, 1):
-        f, m = at[ORDERS[p][0]], at[ORDERS[p][1]]
-        for off in (1, 2, 3):
-            ring2(p, off).wait_recv()
-        g2[p] = (
-            g1[p, m] + rb2[p, 0].astype(F32) + rb2[p, 1].astype(F32) + rb2[p, 2].astype(F32)
-        ).reshape(4, ROWS, WIDTH)
-        for off in (1, 2, 3):
-            sb3[p, off - 1] = g2[p, (f + off) % 4]
-            ring3(p, off).start()
-    for p in (0, 1):
-        f, m, l = (at[a] for a in ORDERS[p])
-        for off in (1, 2, 3):
-            ring3(p, off).wait_recv()
-        grad_unit = g2[p, f] + rb3[p, 0] + rb3[p, 1] + rb3[p, 2]
+        l, m, f = place(p)
+
+        def arrive(j, _):
+            ring2(p, j).wait_recv()
+            return 0
+
+        lax.fori_loop(1, 16, arrive, 0)
+        grad_unit = g1[p, m * 4 + f]
+        for j in range(15):
+            grad_unit = grad_unit + rb2[p, j].astype(F32)
         values = batch_ref[pl.ds(p * ROWS, ROWS), :].astype(F32)
         radius = jnp.sqrt(jnp.sum(values * values, axis=1, keepdims=True) + 1e-06)
         unit = values / radius
         along = jnp.sum(unit * grad_unit, axis=1, keepdims=True)
-        mine = pl.ds(p * ROWS, ROWS)
-        grad_ref[mine, :] = (grad_unit - unit * along) / radius
-        own = pl.ds(pl.multiple_of((m * 4 + f) * ROWS, ROWS), ROWS)
-        loss_ref[mine, :] = jnp.log(den[p, l, 1, own, :]) / 2.0 + jnp.log(den[p, l, 0, own, :]) / 50.0
+        grad_ref[pl.ds(p * ROWS, ROWS), :] = (grad_unit - unit * along) / radius
 
     for copy in trade:
         copy.wait_recv()
@@ -366,13 +471,26 @@
 
     for copy in swaps + trade:
         copy.wait_send()
-    for p in (0, 1):
-        for off in (1, 2, 3):
-            for phase in range(3):
-                for copy in gather(p, phase, off, False):
-                    copy.wait_send()
-            for ring in (ring1, ring2, ring3):
-                ring(p, off).wait_send()
+    lax.fori_loop(1, 16, plane_sent, 0)
+
+    def sent(j, _):
+        sums_plane(j).wait_send()
+        for p in (0, 1):
+            ring2(p, j).wait_send()
+        return 0
+
+    lax.fori_loop(1, 16, sent, 0)
+    for off in (1, 2, 3):
+        sums_line(off).wait_send()
+        for p in (0, 1):
+            line_labels(p, off, False).wait_send()
+    for off in (1, 3):
+        for p in (0, 1):
+            line_rows(p, off, False).wait_send()
+            relay(p, off, False).wait_send()
+            onward(p, off).wait_send()
+            for half in (0, 1):
+                ring1(p, off, half).wait_send()
 
 
 def finish(
@@ -442,27 +560,28 @@
             pltpu.VMEM((2, 4, CHUNK, 128), F32),
             pltpu.VMEM((2, 4, CHUNK, KEYS), BF16),
             pltpu.VMEM((2, CHUNK, 128), F32),
-            pltpu.VMEM((4, 2, 4, 4, 128), F32),
-            pltpu.VMEM((3, 3, 2, 4, 4, 128), F32),
+            pltpu.VMEM((3, 2, 4, 4, 128), F32),
+            pltpu.VMEM((15, 2, 4, 4, 128), F32),
+            pltpu.VMEM((3, 2, 4, 4, 128), F32),
             pltpu.VMEM((2, 4, 2, CHUNK, 128), F32),
             pltpu.VMEM((2, 3, CHUNK, WIDTH), F32),
             pltpu.VMEM((2, CHUNK, WIDTH), F32),
-            pltpu.VMEM((2, 3, CHUNK, WIDTH), BF16),
-            pltpu.VMEM((2, 3, CHUNK, WIDTH), BF16),
-            pltpu.VMEM((2, 4, 64, WIDTH), F32),
-            pltpu.VMEM((2, 3, 64, WIDTH), BF16),
-            pltpu.VMEM((2, 3, 64, WIDTH), BF16),
-            pltpu.VMEM((2, 4, ROWS, WIDTH), F32),
-            pltpu.VMEM((2, 3, ROWS, WIDTH), F32),
-            pltpu.VMEM((2, 3, ROWS, WIDTH), F32),
+            pltpu.VMEM((2, 3, 2, 128, WIDTH), BF16),
+            pltpu.VMEM((2, 2, 2, 128, WIDTH), BF16),
+            pltpu.VMEM((2, 2, 128, WIDTH), BF16),
+            pltpu.VMEM((2, 2, 128, WIDTH), F32),
+            pltpu.VMEM((2, 16, ROWS, WIDTH), F32),
+            pltpu.VMEM((2, 16, ROWS, WIDTH), BF16),
+            pltpu.VMEM((2, 15, ROWS, WIDTH), BF16),
             pltpu.VMEM((2 * ROWS, WIDTH), BF16),
             pltpu.VMEM((2 * ROWS, WIDTH), BF16),
             pltpu.VMEM((1, 128), I32),
             pltpu.VMEM((1, 128), I32),
             dma,
-            dma((2, 3, 3)), dma((2, 3, 3)), dma((2, 3, 3)), dma((2, 3, 3)),
-            dma((3, 3)), dma((3, 3)),
-            dma((2, 3, 3)), dma((2, 3, 3)),
+            dma((2, 15)), dma((2, 15)), dma((2, 15)), dma((2, 15)),
+            dma((2, 2)), dma((2, 2)), dma((2, 3)), dma((2, 3)), dma((2, 2)), dma((2, 2)),
+            dma((15,)), dma((15,)), dma((3,)), dma((3,)),
+            dma((2, 2)), dma((2, 2)), dma((2, 2, 2)), dma((2, 2, 2)), dma((2, 15)), dma((2, 15)),
             dma((3,)), dma((3,)), dma((2,)), dma((2,)),
         ],
         compiler_params=pltpu.CompilerParams(

time: 78.9 us -> 73.6 us (0.933)
  Pallas kernels: 77.3 us -> 71.8 us
    pallas_call x1, Pallas kernels: 73.4 us -> 67.9 us  [per_device(): pl.pallas_call(kernel, out_shape=(jax.ShapeDtypeStruct((local_rows, WIDTH...]
where the time goes in v3:
time: 73.6 us; the launch traced here: 73.1 us
  Pallas kernels  71.8 us (98%)
  between operations  1.29 us (2%)
    pallas_call x1, Pallas kernels, per_device(): pl.pallas_call(kernel, out_shape=(jax.ShapeDtypeStruct((local_rows, WIDTH...  67.9 us
    pallas_call x1, Pallas kernels, per_device(): pl.pallas_call(finish, out_shape=(jax.ShapeDtypeStruct((local_rows, WIDTH...  3.92 us

profile of v3, /device:TPU:0, one launch (start us, length us, event | category | flops | bytes accessed | tf_op | source)
XLA Modules:
  0.0 73.1 jit_solution(17706659668790853890)
XLA Ops:
  1.3 67.9 %xbm.1 = (f32[32,512]{1,0:T(8,128)}, f32[32,128]{1,0:T(8,128)}, bf16[32,512]{1,0:T(8,128)(2,1)}, s32[1,128]{1,0:T(1,128)}) custom-call(s32[1]{0:T(128)S(6)} %copy.10.step_ref, bf16[32,512]{1,0:T(8,128)(2,1)} %batch_ref.1, s32[1,32]{1,0:T(1,128)} %bitcast.8, s32[1,2048]{1,0:T(1,128)} %bitcast.5, s32[1,2048]{1,0:T(1,128)} %bitcast.7, bf16[2048,512]{1,0:T(8,128)(2,1)} %mem_ref.3), custom_call_target="tpu_custom_call" | custom-call | tf_op jit(solution)/shard_map/xbm/pallas_call | solution.py:541
  69.2 3.9 %finish.1 = (f32[32,512]{1,0:T(8,128)}, f32[1,32]{1,0:T(1,128)}, s32[1,2048]{1,0:T(1,128)}, bf16[2048,512]{1,0:T(8,128)(2,1)}) custom-call(s32[1]{0:T(128)S(6)} %copy.10.step_ref, f32[32,512]{1,0:T(8,128)} %get-tuple-element.12.grad_ref, f32[32,128]{1,0:T(8,128)} %get-tuple-element.13.loss_ref, bf16[32,512]{1,0:T(8,128)(2,1)} %get-tuple-element.14.moved_ref, ...), custom_call_target="tpu_custom_call" | custom-call | tf_op jit(solution)/shard_map/finish/pallas_call | solution.py:601

commit v4 on v3

--- a/solution.py
+++ b/solution.py
@@ -19,6 +19,7 @@
 WIDTH = 512
 KEYS_DEV = 2048
 KEYS = 4096
+OTHERS = (10, 6, 14, 9, 11, 2, 8, 5, 7, 13, 15, 1, 3, 4, 12)
 SLOTS = KEYS_DEV // (2 * ROWS)
 
 
@@ -31,11 +32,12 @@
 
 
 def kernel(
-    step_ref, batch_ref, blab_ref, mlab_ref, keep_ref, mem_ref,
+    step_hbm, batch_hbm, blab_hbm, mlab_ref, keep_ref, mem_ref,
     grad_ref, loss_ref, moved_ref, mvlab_ref,
+    step_ref, batch_ref, blab_ref,
     mraw, klraw, kpraw, keys, klab, raw, labs, an, labc, terms, acc, sums, sums_in, sums_z, den,
     pair, gown, sb1, rb1, hb, gr, g1, sb2, rb2, cand, cand_in, clab, clab_in,
-    mem_sem, pl_s, pl_r, pll_s, pll_r, ln_s, ln_r, lnl_s, lnl_r, fw_s, fw_r,
+    mem_sem, in_sem, pl_s, pl_r, pll_s, pll_r, ln_s, ln_r, lnl_s, lnl_r, fw_s, fw_r,
     as_s, as_r, az_s, az_r, h1_s, h1_r, r1_s, r1_r, r2_s, r2_r, pt_s, pt_r, bt_s, bt_r,
 ):
     n_dev = lax.axis_size("dev")
@@ -47,22 +49,34 @@
     def device(index):
         return (index // n_dev, index % n_dev)
 
+    even = core == 0
+    sx, sy, sz = ([(at[a] + d) % 4 for d in range(4)] for a in range(3))
+    grp_x, grp_y = [2 * v for v in sx], [v // 2 for v in sy]
+    dev_y, dev_z = [8 * (v % 2) for v in sy], [2 * v + core for v in sz]
+    along_x = [(grp_x[d] + grp_y[0], dev_y[0]) for d in range(4)]
+    along_y = [(grp_x[0] + grp_y[d], dev_y[d]) for d in range(4)]
+    mid1 = [tuple(jnp.where(even, a, b) for a, b in zip(along_x[d], along_y[d])) for d in range(4)]
+    last1 = [tuple(jnp.where(even, a, b) for a, b in zip(along_y[d], along_x[d])) for d in range(4)]
+    places = (
+        (sz, sy, sx),
+        ([jnp.where(even, a, b) for a, b in zip(sy, sx)], [jnp.where(even, a, b) for a, b in zip(sx, sy)], sz),
+    )
+
     def chip_at(dx, dy, dz):
-        there = ((at[0] + dx) % 4) * 16 + ((at[1] + dy) % 4) * 4 + (at[2] + dz) % 4
-        return device(2 * there + core)
+        return grp_x[dx] + grp_y[dy], dev_y[dy] + dev_z[dz]
 
     def peer(p, dl, dm, df):
-        first, even = p == 0, core == 0
-        dx = jnp.where(first, df, jnp.where(even, dm, dl))
-        dy = jnp.where(first, dm, jnp.where(even, dl, dm))
-        dz = jnp.where(first, dl, df)
-        return chip_at(dx, dy, dz)
+        if not isinstance(p, int):
+            return tuple(jnp.where(p == 0, a, b) for a, b in zip(peer(0, dl, dm, df), peer(1, dl, dm, df)))
+        if p == 0:
+            return chip_at(df, dm, dl)
+        grp, dev = last1[dl] if dl else mid1[dm]
+        return grp, dev + dev_z[df]
 
     def place(p):
-        first, even = p == 0, core == 0
-        last = jnp.where(first, at[2], jnp.where(even, at[1], at[0]))
-        middle = jnp.where(first, at[1], jnp.where(even, at[0], at[1]))
-        return last, middle, jnp.where(first, at[0], at[2])
+        if isinstance(p, int):
+            return tuple(axis[0] for axis in places[p])
+        return tuple(jnp.where(p == 0, a[0], b[0]) for a, b in zip(*places))
 
     partner = device(me + 1 - 2 * core)
 
@@ -73,60 +87,72 @@
 
     own_mem = pltpu.make_async_copy(mem_ref, mraw.at[0], mem_sem)
     own_mem.start()
+    small = (
+        pltpu.make_async_copy(blab_hbm, blab_ref, in_sem.at[0]),
+        pltpu.make_async_copy(batch_hbm, batch_ref, in_sem.at[1]),
+        pltpu.make_async_copy(step_hbm, step_ref, in_sem.at[2]),
+        pltpu.make_async_copy(mlab_ref, klraw.at[0], in_sem.at[3]),
+        pltpu.make_async_copy(keep_ref, kpraw.at[0], in_sem.at[4]),
+    )
+    blocks = []
+    for p in (0, 1):
+        l, m, f = place(p)
+        blocks.append(
+            pltpu.make_async_copy(
+                batch_hbm.at[pl.ds(p * ROWS, ROWS)], raw.at[p, l, m, f], in_sem.at[5 + p]
+            )
+        )
+    for copy in (*small, *blocks):
+        copy.start()
 
     barrier = pltpu.get_barrier_semaphore()
     def greet(p, dl, dm, df):
         pl.semaphore_signal(barrier, inc=1, device_id=peer(p, dl, dm, df), device_id_type=MESH)
 
-    def greet_plane(j, _):
+    for j in OTHERS:
         greet(0, 0, j // 4, j % 4)
-        return 0
-
-    def greet_diagonal(j, _):
-        greet(1, 0, 1 + j // 3, 1 + j % 3)
-        return 0
-
-    lax.fori_loop(1, 16, greet_plane, 0)
-    lax.fori_loop(0, 9, greet_diagonal, 0)
+    for j in OTHERS:
+        if j // 4 and j % 4:
+            greet(1, 0, j // 4, j % 4)
     for off in (1, 2, 3):
         greet(0, off, 0, 0)
     pl.semaphore_signal(barrier, inc=1, device_id=partner, device_id_type=MESH)
+    for copy in (*small, *blocks):
+        copy.wait()
     for i in range(4):
         clab[:, 2 * ROWS * i : 2 * ROWS * (i + 1)] = blab_ref[...]
     for p in (0, 1):
         l, m, f = place(p)
-        raw[p, l, m, f] = batch_ref[pl.ds(p * ROWS, ROWS), :]
         labs[p, l, m, f] = clab[...]
     pl.semaphore_wait(barrier, 28)
 
     def to_plane(p, j, back):
-        l, m, f = place(p)
         dm, df = j // 4, j % 4
-        if back:
-            m, f = (m + 4 - dm) % 4, (f + 4 - df) % 4
+        l, middle, first = places[p][0][0], places[p][1], places[p][2]
+        m, f = (middle[-dm % 4], first[-df % 4]) if back else (middle[0], first[0])
         rows, labels, to = raw.at[p, l, m, f], labs.at[p, l, m, f], peer(p, 0, dm, df)
         return (
             remote(rows, rows, pl_s.at[p, j - 1], pl_r.at[p, j - 1], to),
             remote(labels, labels, pll_s.at[p, j - 1], pll_r.at[p, j - 1], to),
         )
 
-    def plane_start(j, _):
-        for p in (0, 1):
-            for copy in to_plane(p, j, False):
-                copy.start()
-        return 0
-
-    def plane_recv(j, _):
-        for p in (0, 1):
-            for copy in to_plane(p, j, True):
-                copy.wait_recv()
-        return 0
-
-    def plane_sent(j, _):
-        for p in (0, 1):
-            for copy in to_plane(p, j, False):
-                copy.wait_send()
-        return 0
+    def plane_start():
+        for j in OTHERS:
+            for p in (0, 1):
+                for copy in to_plane(p, j, False):
+                    copy.start()
+
+    def plane_recv():
+        for j in OTHERS:
+            for p in (0, 1):
+                for copy in to_plane(p, j, True):
+                    copy.wait_recv()
+
+    def plane_sent():
+        for j in OTHERS:
+            for p in (0, 1):
+                for copy in to_plane(p, j, False):
+                    copy.wait_send()
 
     def line_rows(p, off, back):
         l = place(p)[0]
@@ -148,7 +174,7 @@
         half = raw.at[p, l, pl.ds(0 if off == 1 else 2, 2)]
         return remote(half, half, fw_s.at[p, off // 2], fw_r.at[p, off // 2], peer(p, off, 0, 0))
 
-    lax.fori_loop(1, 16, plane_start, 0)
+    plane_start()
     swaps = (
         remote(mem_ref, mraw.at[1], pt_s.at[0], pt_r.at[0], partner),
         remote(mlab_ref, klraw.at[1], pt_s.at[1], pt_r.at[1], partner),
@@ -156,9 +182,6 @@
     )
     for copy in swaps:
         copy.start()
-
-    klraw[0] = mlab_ref[...]
-    kpraw[0] = keep_ref[...]
 
     def normalize_memory(half):
         def block(i, _):
@@ -176,7 +199,7 @@
 
     own_mem.wait()
     normalize_memory(0)
-    lax.fori_loop(1, 16, plane_recv, 0)
+    plane_recv()
     for p in (1, 0):
         for off in (1, 3):
             line_rows(p, off, False).start()
@@ -275,21 +298,15 @@
     def add_up(i, _):
         @pl.when(i == 0)
         def _():
-            def begin(j, _):
+            for j in OTHERS:
                 sums_plane(j).start()
-                return 0
-
-            lax.fori_loop(1, 16, begin, 0)
 
         alone(i)
 
         @pl.when(i == 1)
         def _():
-            def arrive(j, _):
+            for j in OTHERS:
                 sums_plane(j).wait_recv()
-                return 0
-
-            lax.fori_loop(1, 16, arrive, 0)
             total = sums[0]
             for j in range(15):
                 total = total + sums_in[j]
@@ -385,9 +402,8 @@
     lax.fori_loop(0, 5, push, 0)
 
     def ring2(p, j):
-        l, m, f = place(p)
         dm, df = j // 4, j % 4
-        block = ((m + dm) % 4) * 4 + (f + df) % 4
+        block = places[p][1][dm] * 4 + places[p][2][df]
         return remote(
             sb2.at[p, block], rb2.at[p, j - 1], r2_s.at[p, j - 1], r2_r.at[p, j - 1], peer(p, 0, dm, df)
         )
@@ -401,11 +417,8 @@
         ).reshape(16, ROWS, WIDTH)
         sb2[p] = g1[p].astype(BF16)
 
-        def begin(j, _):
+        for j in OTHERS:
             ring2(p, j).start()
-            return 0
-
-        lax.fori_loop(1, 16, begin, 0)
 
     step = step_ref[0]
     odd = step % 2
@@ -449,11 +462,8 @@
     for p in (0, 1):
         l, m, f = place(p)
 
-        def arrive(j, _):
+        for j in OTHERS:
             ring2(p, j).wait_recv()
-            return 0
-
-        lax.fori_loop(1, 16, arrive, 0)
         grad_unit = g1[p, m * 4 + f]
         for j in range(15):
             grad_unit = grad_unit + rb2[p, j].astype(F32)
@@ -471,15 +481,12 @@
 
     for copy in swaps + trade:
         copy.wait_send()
-    lax.fori_loop(1, 16, plane_sent, 0)
-
-    def sent(j, _):
+    plane_sent()
+
+    for j in OTHERS:
         sums_plane(j).wait_send()
         for p in (0, 1):
             ring2(p, j).wait_send()
-        return 0
-
-    lax.fori_loop(1, 16, sent, 0)
     for off in (1, 2, 3):
         sums_line(off).wait_send()
         for p in (0, 1):
@@ -494,11 +501,11 @@
 
 
 def finish(
-    step_ref, grad_ref, loss_ref, moved_ref, mvlab_ref, mlab_ref, mem_ref,
-    grad_out, loss_out, lab_out, mem_out, buf, sem_in, sem_out,
+    step_hbm, grad_hbm, loss_hbm, moved_hbm, mvlab_hbm, mlab_hbm, mem_ref,
+    grad_out, loss_out, lab_out, mem_out,
+    step_ref, grad, loss_in, moved, mvlab, mlab, loss, labels, buf, small_sem, done_sem, sem_in, sem_out,
 ):
     pieces, size = buf.shape[0], buf.shape[1]
-    slot = step_ref[0] % SLOTS
     loads = [
         pltpu.make_async_copy(mem_ref.at[pl.ds(i * size, size)], buf.at[i], sem_in.at[i])
         for i in range(pieces)
@@ -507,35 +514,51 @@
         pltpu.make_async_copy(buf.at[i], mem_out.at[pl.ds(i * size, size)], sem_out.at[i])
         for i in range(pieces)
     ]
-    for load in loads:
-        load.start()
-    grad_out[...] = grad_ref[...]
-    rows = loss_ref.shape[0]
+    pairs = (
+        (step_hbm, step_ref), (moved_hbm, moved), (mvlab_hbm, mvlab), (mlab_hbm, mlab),
+        (loss_hbm, loss_in), (grad_hbm, grad),
+    )
+    small = [pltpu.make_async_copy(a, b, small_sem.at[i]) for i, (a, b) in enumerate(pairs)]
+    results = [
+        pltpu.make_async_copy(a, b, done_sem.at[i])
+        for i, (a, b) in enumerate(((loss, loss_out), (labels, lab_out), (grad, grad_out)))
+    ]
+    for copy in (*small[:2], *loads, *small[2:]):
+        copy.start()
+    small[0].wait()
+    small[1].wait()
+    slot = step_ref[0] % SLOTS
+    per_piece = size // (2 * ROWS)
+    for i in range(pieces):
+        loads[i].wait()
+
+        @pl.when(slot // per_piece == i)
+        def _():
+            at = pl.multiple_of((slot % per_piece) * (2 * ROWS), 2 * ROWS)
+            buf[i, pl.ds(at, 2 * ROWS), :] = moved[...]
+
+        stores[i].start()
+    for copy in small[2:]:
+        copy.wait()
+    results[2].start()
+    rows = loss_in.shape[0]
     diagonal = lax.broadcasted_iota(I32, (rows, 128), 0) == lax.broadcasted_iota(I32, (rows, 128), 1)
-    loss_out[...] = jnp.sum(jnp.where(diagonal, loss_ref[...], 0.0), axis=0, keepdims=True)[:, :rows]
+    loss[...] = jnp.sum(jnp.where(diagonal, loss_in[...], 0.0), axis=0, keepdims=True)[:, :rows]
+    results[0].start()
     lane = lax.broadcasted_iota(I32, (1, 128), 1) // (2 * ROWS)
     for i in range(KEYS_DEV // 128):
         here = pl.ds(i * 128, 128)
-        lab_out[:, here] = jnp.where(
-            lane + i * (64 // ROWS) == jnp.full((1, 128), slot, I32), mvlab_ref[...], mlab_ref[:, here]
-        )
-    per_piece = size // (2 * ROWS)
-    for i in range(pieces):
-        loads[i].wait()
-
-        @pl.when(slot // per_piece == i)
-        def _():
-            at = pl.multiple_of((slot % per_piece) * (2 * ROWS), 2 * ROWS)
-            buf[i, pl.ds(at, 2 * ROWS), :] = moved_ref[...]
-
-        stores[i].start()
-    for store in stores:
-        store.wait()
+        labels[:, here] = jnp.where(
+            lane + i * (64 // ROWS) == jnp.full((1, 128), slot, I32), mvlab[...], mlab[:, here]
+        )
+    results[1].start()
+    for copy in (*stores, *results):
+        copy.wait()
 
 
 def per_device(batch_rows, batch_labels, memory, memory_labels, keep_bits, step_index):
     local_rows = batch_rows.shape[0]
-    vmem = pl.BlockSpec(memory_space=pltpu.VMEM)
+    vmem, hbm = pl.BlockSpec(memory_space=pltpu.VMEM), pl.BlockSpec(memory_space=pl.ANY)
     dma = pltpu.SemaphoreType.DMA
     memory_labels_row = memory_labels.reshape(1, KEYS_DEV)
     grad, loss, moved, moved_labels = pl.pallas_call(
@@ -546,9 +569,12 @@
             jax.ShapeDtypeStruct((local_rows, WIDTH), BF16),
             jax.ShapeDtypeStruct((1, 128), I32),
         ),
-        in_specs=[pl.BlockSpec(memory_space=pltpu.SMEM), vmem, vmem, vmem, vmem, pl.BlockSpec(memory_space=pl.ANY)],
+        in_specs=[hbm] * 6,
         out_specs=(vmem, vmem, vmem, vmem),
         scratch_shapes=[
+            pltpu.SMEM((1,), I32),
+            pltpu.VMEM((2 * ROWS, WIDTH), BF16),
+            pltpu.VMEM((1, 2 * ROWS), I32),
             pltpu.VMEM((2, KEYS_DEV, WIDTH), BF16),
             pltpu.VMEM((2, 1, KEYS_DEV), I32),
             pltpu.VMEM((2, 1, KEYS_DEV), I32),
@@ -578,6 +604,7 @@
             pltpu.VMEM((1, 128), I32),
             pltpu.VMEM((1, 128), I32),
             dma,
+            dma((7,)),
             dma((2, 15)), dma((2, 15)), dma((2, 15)), dma((2, 15)),
             dma((2, 2)), dma((2, 2)), dma((2, 3)), dma((2, 3)), dma((2, 2)), dma((2, 2)),
             dma((15,)), dma((15,)), dma((3,)), dma((3,)),
@@ -596,7 +623,6 @@
         keep_bits.reshape(1, KEYS_DEV),
         memory,
     )
-    smem, hbm = pl.BlockSpec(memory_space=pltpu.SMEM), pl.BlockSpec(memory_space=pl.ANY)
     pieces = 4
     grad, loss_row, new_labels, new_memory = pl.pallas_call(
         finish,
@@ -606,10 +632,19 @@
             jax.ShapeDtypeStruct((1, KEYS_DEV), I32),
             jax.ShapeDtypeStruct((KEYS_DEV, WIDTH), BF16),
         ),
-        in_specs=[smem, vmem, vmem, vmem, vmem, vmem, hbm],
-        out_specs=(vmem, vmem, vmem, hbm),
+        in_specs=[hbm] * 7,
+        out_specs=(hbm,) * 4,
         scratch_shapes=[
-            pltpu.VMEM((pieces, KEYS_DEV // pieces, WIDTH), BF16), dma((pieces,)), dma((pieces,)),
+            pltpu.SMEM((1,), I32),
+            pltpu.VMEM((local_rows, WIDTH), F32),
+            pltpu.VMEM((local_rows, 128), F32),
+            pltpu.VMEM((local_rows, WIDTH), BF16),
+            pltpu.VMEM((1, 128), I32),
+            pltpu.VMEM((1, KEYS_DEV), I32),
+            pltpu.VMEM((1, local_rows), F32),
+            pltpu.VMEM((1, KEYS_DEV), I32),
+            pltpu.VMEM((pieces, KEYS_DEV // pieces, WIDTH), BF16),
+            dma((6,)), dma((3,)), dma((pieces,)), dma((pieces,)),
         ],
         name="finish",
     )(step_index, grad, loss, moved, moved_labels, memory_labels_row, memory)

time: 73.6 us -> 70.8 us (0.962)
  Pallas kernels: 71.8 us -> 69.4 us
    pallas_call x1, Pallas kernels: 3.92 us -> 2.54 us  [per_device(): pl.pallas_call(finish, out_shape=(jax.ShapeDtypeStruct((local_rows, WIDTH...]
    pallas_call x1, Pallas kernels: 67.9 us -> 66.8 us  [per_device(): pl.pallas_call(kernel, out_shape=(jax.ShapeDtypeStruct((local_rows, WIDTH...]
where the time goes in v4:
time: 70.8 us; the launch traced here: 70.7 us
  Pallas kernels  69.4 us (98%)
  between operations  1.29 us (2%)
    pallas_call x1, Pallas kernels, per_device(): pl.pallas_call(kernel, out_shape=(jax.ShapeDtypeStruct((local_rows, WIDTH...  66.8 us
    pallas_call x1, Pallas kernels, per_device(): pl.pallas_call(finish, out_shape=(jax.ShapeDtypeStruct((local_rows, WIDTH...  2.54 us

profile of v4, /device:TPU:0, one launch (start us, length us, event | category | flops | bytes accessed | tf_op | source)
XLA Modules:
  0.0 70.7 jit_solution(14277337825513892248)
XLA Ops:
  1.3 66.8 %xbm.1 = (f32[32,512]{1,0:T(8,128)}, f32[32,128]{1,0:T(8,128)}, bf16[32,512]{1,0:T(8,128)(2,1)}, s32[1,128]{1,0:T(1,128)}) custom-call(s32[1]{0:T(128)S(6)} %copy.10.step_hbm, bf16[32,512]{1,0:T(8,128)(2,1)} %batch_hbm.1, s32[1,32]{1,0:T(1,128)} %bitcast.8, s32[1,2048]{1,0:T(1,128)} %bitcast.5, s32[1,2048]{1,0:T(1,128)} %bitcast.7, bf16[2048,512]{1,0:T(8,128)(2,1)} %mem_ref.3), custom_call_target="tpu_custom_call" | custom-call | tf_op jit(solution)/shard_map/xbm/pallas_call | solution.py:564
  68.1 2.5 %finish.1 = (f32[32,512]{1,0:T(8,128)}, f32[1,32]{1,0:T(1,128)}, s32[1,2048]{1,0:T(1,128)}, bf16[2048,512]{1,0:T(8,128)(2,1)}) custom-call(s32[1]{0:T(128)S(6)} %copy.10.step_hbm, f32[32,512]{1,0:T(8,128)} %get-tuple-element.12.grad_hbm, f32[32,128]{1,0:T(8,128)} %get-tuple-element.13.loss_hbm, bf16[32,512]{1,0:T(8,128)(2,1)} %get-tuple-element.14.moved_hbm, ...), custom_call_target="tpu_custom_call" | custom-call | tf_op jit(solution)/shard_map/finish/pallas_call | solution.py:627

commit v5 on v4

--- a/solution.py
+++ b/solution.py
@@ -195,19 +195,19 @@
             keys[pl.ds(pl.multiple_of(half * KEYS_DEV + row, 128), 128), :] = (values * scale).astype(BF16)
             return 0
 
-        lax.fori_loop(0, KEYS_DEV // 128, block, 0)
+        lax.fori_loop(0, KEYS_DEV // 128, block, 0, unroll=4)
 
     own_mem.wait()
     normalize_memory(0)
+    for copy in swaps:
+        copy.wait_recv()
+    normalize_memory(1)
     plane_recv()
     for p in (1, 0):
         for off in (1, 3):
             line_rows(p, off, False).start()
         for off in (1, 3, 2):
             line_labels(p, off, False).start()
-    for copy in swaps:
-        copy.wait_recv()
-    normalize_memory(1)
 
     dropped = float(KEYS) - jnp.sum(
         jnp.where(kpraw[...] > 0, 1.0, 0.0).reshape(2, KEYS_DEV), axis=(0, 1), keepdims=True

time: 70.8 us -> 69 us (0.975)
  the two profiles are of different devices: /device:TPU:0 before, /device:TPU:24 now
where the time goes in v5:
time: 69 us; the launch traced here: 68.8 us
  Pallas kernels  67.5 us (98%)
  between operations  1.29 us (2%)
    pallas_call x1, Pallas kernels, per_device(): pl.pallas_call(kernel, out_shape=(jax.ShapeDtypeStruct((local_rows, WIDTH...  65 us
    pallas_call x1, Pallas kernels, per_device(): pl.pallas_call(finish, out_shape=(jax.ShapeDtypeStruct((local_rows, WIDTH...  2.53 us

profile of v5, /device:TPU:24, one launch (start us, length us, event | category | flops | bytes accessed | tf_op | source)
XLA Modules:
  0.0 68.8 jit_solution(18180980697359832250)
XLA Ops:
  1.3 65.0 %xbm.1 = (f32[32,512]{1,0:T(8,128)}, f32[32,128]{1,0:T(8,128)}, bf16[32,512]{1,0:T(8,128)(2,1)}, s32[1,128]{1,0:T(1,128)}) custom-call(s32[1]{0:T(128)S(6)} %copy.10.step_hbm, bf16[32,512]{1,0:T(8,128)(2,1)} %batch_hbm.1, s32[1,32]{1,0:T(1,128)} %bitcast.8, s32[1,2048]{1,0:T(1,128)} %bitcast.5, s32[1,2048]{1,0:T(1,128)} %bitcast.7, bf16[2048,512]{1,0:T(8,128)(2,1)} %mem_ref.3), custom_call_target="tpu_custom_call" | custom-call | tf_op jit(solution)/shard_map/xbm/pallas_call | solution.py:564
  66.2 2.5 %finish.1 = (f32[32,512]{1,0:T(8,128)}, f32[1,32]{1,0:T(1,128)}, s32[1,2048]{1,0:T(1,128)}, bf16[2048,512]{1,0:T(8,128)(2,1)}) custom-call(s32[1]{0:T(128)S(6)} %copy.10.step_hbm, f32[32,512]{1,0:T(8,128)} %get-tuple-element.12.grad_hbm, f32[32,128]{1,0:T(8,128)} %get-tuple-element.13.loss_hbm, bf16[32,512]{1,0:T(8,128)(2,1)} %get-tuple-element.14.moved_hbm, ...), custom_call_target="tpu_custom_call" | custom-call | tf_op jit(solution)/shard_map/finish/pallas_call | solution.py:627

commit v6 on v5

--- a/solution.py
+++ b/solution.py
@@ -174,16 +174,22 @@
         half = raw.at[p, l, pl.ds(0 if off == 1 else 2, 2)]
         return remote(half, half, fw_s.at[p, off // 2], fw_r.at[p, off // 2], peer(p, off, 0, 0))
 
-    plane_start()
+    halves = tuple(
+        remote(
+            mem_ref.at[pl.ds(h * 1024, 1024)], mraw.at[1, pl.ds(h * 1024, 1024)],
+            pt_s.at[3 * h], pt_r.at[3 * h], partner,
+        )
+        for h in (0, 1)
+    )
     swaps = (
-        remote(mem_ref, mraw.at[1], pt_s.at[0], pt_r.at[0], partner),
         remote(mlab_ref, klraw.at[1], pt_s.at[1], pt_r.at[1], partner),
         remote(keep_ref, kpraw.at[1], pt_s.at[2], pt_r.at[2], partner),
     )
-    for copy in swaps:
+    for copy in swaps + halves:
         copy.start()
-
-    def normalize_memory(half):
+    plane_start()
+
+    def normalize_memory(half, begin, end):
         def block(i, _):
             row = pl.multiple_of(i * 128, 128)
             kept = kpraw[half, :, pl.ds(row, 128)] > 0
@@ -195,13 +201,16 @@
             keys[pl.ds(pl.multiple_of(half * KEYS_DEV + row, 128), 128), :] = (values * scale).astype(BF16)
             return 0
 
-        lax.fori_loop(0, KEYS_DEV // 128, block, 0, unroll=4)
+        lax.fori_loop(begin, end, block, 0, unroll=8)
 
     own_mem.wait()
-    normalize_memory(0)
+    normalize_memory(0, 0, 16)
     for copy in swaps:
         copy.wait_recv()
-    normalize_memory(1)
+    halves[0].wait_recv()
+    normalize_memory(1, 0, 8)
+    halves[1].wait_recv()
+    normalize_memory(1, 8, 16)
     plane_recv()
     for p in (1, 0):
         for off in (1, 3):
@@ -479,7 +488,7 @@
     moved_ref[...] = jnp.where(keep_mine, cand[...].astype(F32), cand_in[...].astype(F32)).astype(BF16)
     mvlab_ref[...] = jnp.where(jnp.full((1, 128), odd, I32) == 0, clab[...], clab_in[...])
 
-    for copy in swaps + trade:
+    for copy in swaps + halves + trade:
         copy.wait_send()
     plane_sent()
 
@@ -609,7 +618,7 @@
             dma((2, 2)), dma((2, 2)), dma((2, 3)), dma((2, 3)), dma((2, 2)), dma((2, 2)),
             dma((15,)), dma((15,)), dma((3,)), dma((3,)),
             dma((2, 2)), dma((2, 2)), dma((2, 2, 2)), dma((2, 2, 2)), dma((2, 15)), dma((2, 15)),
-            dma((3,)), dma((3,)), dma((2,)), dma((2,)),
+            dma((4,)), dma((4,)), dma((2,)), dma((2,)),
         ],
         compiler_params=pltpu.CompilerParams(
             collective_id=0, has_side_effects=True, vmem_limit_bytes=60 * 1024 * 1024

time: 69 us -> 68.9 us (level)
  the two profiles are of different devices: /device:TPU:24 before, /device:TPU:0 now
where the time goes in v6:
time: 68.9 us; the launch traced here: 68.3 us
  Pallas kernels  67 us (97%)
  between operations  1.29 us (2%)
    pallas_call x1, Pallas kernels, per_device(): pl.pallas_call(kernel, out_shape=(jax.ShapeDtypeStruct((local_rows, WIDTH...  64.5 us
    pallas_call x1, Pallas kernels, per_device(): pl.pallas_call(finish, out_shape=(jax.ShapeDtypeStruct((local_rows, WIDTH...  2.54 us

profile of v6, /device:TPU:0, one launch (start us, length us, event | category | flops | bytes accessed | tf_op | source)
XLA Modules:
  0.0 68.3 jit_solution(6093898163927388589)
XLA Ops:
  1.3 64.5 %xbm.1 = (f32[32,512]{1,0:T(8,128)}, f32[32,128]{1,0:T(8,128)}, bf16[32,512]{1,0:T(8,128)(2,1)}, s32[1,128]{1,0:T(1,128)}) custom-call(s32[1]{0:T(128)S(6)} %copy.10.step_hbm, bf16[32,512]{1,0:T(8,128)(2,1)} %batch_hbm.1, s32[1,32]{1,0:T(1,128)} %bitcast.8, s32[1,2048]{1,0:T(1,128)} %bitcast.5, s32[1,2048]{1,0:T(1,128)} %bitcast.7, bf16[2048,512]{1,0:T(8,128)(2,1)} %mem_ref.3), custom_call_target="tpu_custom_call" | custom-call | tf_op jit(solution)/shard_map/xbm/pallas_call | solution.py:573
  65.8 2.5 %finish.1 = (f32[32,512]{1,0:T(8,128)}, f32[1,32]{1,0:T(1,128)}, s32[1,2048]{1,0:T(1,128)}, bf16[2048,512]{1,0:T(8,128)(2,1)}) custom-call(s32[1]{0:T(128)S(6)} %copy.10.step_hbm, f32[32,512]{1,0:T(8,128)} %get-tuple-element.12.grad_hbm, f32[32,128]{1,0:T(8,128)} %get-tuple-element.13.loss_hbm, bf16[32,512]{1,0:T(8,128)(2,1)} %get-tuple-element.14.moved_hbm, ...), custom_call_target="tpu_custom_call" | custom-call | tf_op jit(solution)/shard_map/finish/pallas_call | solution.py:636
